TPU v7x, 128 devices: a whole 4x4x4 slice. The times are simulated.
128 devices in a mesh: dp: 16 (over x, z), mp: 8 (over y, core).
Axes of the slice: x: 4, y: 4, z: 4, core: 2. Of those that a mesh axis runs over, the one named last changes fastest.
Arguments:
- inputs: int32 [64, 512], P('dp'), may hold values from 0 to 255
- targets: int32 [64, 512], P('dp'), may hold values from 0 to 255
- valid_mask: int32 [64, 512], P('dp'), may hold values from 0 to 1
- memory: bfloat16 [2, 64, 512, 512], P(None, 'dp'), may hold values from -6 to 6
- attention_rank: int32 [2, 5, 8, 8], P(None, None, None, 'mp'), may hold values from 0 to 9
- feedforward_rank: int32 [2, 2, 8, 32], P(None, None, None, 'mp'), may hold values from 0 to 9
- attention_weight: float32 [2, 5, 512, 512], P(None, None, None, 'mp'), may hold values from -0.25 to 0.25
- attention_moment: float32 [2, 5, 512, 512], P(None, None, None, 'mp'), may hold values from -0.0034179688 to 0.0034179688
- attention_average: float32 [2, 5, 512, 512], P(None, None, None, 'mp'), may hold values from -0.25 to 0.25
- feedforward_weight: float32 [2, 2, 512, 2048], P(None, None, None, 'mp'), may hold values from -0.625 to 0.625
- feedforward_moment: float32 [2, 2, 512, 2048], P(None, None, None, 'mp'), may hold values from -0.0034179688 to 0.0034179688
- feedforward_average: float32 [2, 2, 512, 2048], P(None, None, None, 'mp'), may hold values from -0.625 to 0.625
- embedding_weight: float32 [256, 512], replicated, may hold values from -8 to 8
- embedding_moment: float32 [256, 512], replicated, may hold values from -0.0034179688 to 0.0034179688
- embedding_average: float32 [256, 512], replicated, may hold values from -8 to 8
- head_bias_weight: float32 [2, 2, 512], P(None, None, 'mp'), may hold values from -1.75 to 1.75
- head_bias_moment: float32 [2, 2, 512], P(None, None, 'mp'), may hold values from -0.0034179688 to 0.0034179688
- head_bias_average: float32 [2, 2, 512], P(None, None, 'mp'), may hold values from -1.75 to 1.75
- inner_bias_weight: float32 [2, 2048], P(None, 'mp'), may hold values from -0.625 to 0.625
- inner_bias_moment: float32 [2, 2048], P(None, 'mp'), may hold values from -0.0034179688 to 0.0034179688
- inner_bias_average: float32 [2, 2048], P(None, 'mp'), may hold values from -0.625 to 0.625
- norm_weight: float32 [2, 5, 512], replicated, as said below
- norm_moment: float32 [2, 5, 512], replicated, may hold values from -0.0034179688 to 0.0034179688
- norm_average: float32 [2, 5, 512], replicated, may hold values from -3 to 3
Outputs:
- ce_total: float32 [], replicated
- valid_count: float32 [], replicated
- new_memory: bfloat16 [2, 64, 512, 512], P(None, 'dp')
- attention_grad: float32 [2, 5, 512, 512], P(None, None, None, 'mp')
- attention_next: float32 [2, 5, 512, 512], P(None, None, None, 'mp')
- attention_moment_next: float32 [2, 5, 512, 512], P(None, None, None, 'mp')
- attention_average_next: float32 [2, 5, 512, 512], P(None, None, None, 'mp')
- feedforward_grad: float32 [2, 2, 512, 2048], P(None, None, None, 'mp')
- feedforward_next: float32 [2, 2, 512, 2048], P(None, None, None, 'mp')
- feedforward_moment_next: float32 [2, 2, 512, 2048], P(None, None, None, 'mp')
- feedforward_average_next: float32 [2, 2, 512, 2048], P(None, None, None, 'mp')
- embedding_next: float32 [256, 512], replicated
- embedding_moment_next: float32 [256, 512], replicated
- embedding_average_next: float32 [256, 512], replicated
- head_bias_next: float32 [2, 2, 512], P(None, None, 'mp')
- head_bias_moment_next: float32 [2, 2, 512], P(None, None, 'mp')
- head_bias_average_next: float32 [2, 2, 512], P(None, None, 'mp')
- inner_bias_next: float32 [2, 2048], P(None, 'mp')
- inner_bias_moment_next: float32 [2, 2048], P(None, 'mp')
- inner_bias_average_next: float32 [2, 2048], P(None, 'mp')
- norm_grad: float32 [2, 5, 512], replicated
- norm_next: float32 [2, 5, 512], replicated
- norm_moment_next: float32 [2, 5, 512], replicated
- norm_average_next: float32 [2, 5, 512], replicated
Inputs may be any that keep to these rules, and one draw needn't show every extreme that they name: `norm_weight`: rows 0 and 2 of each layer are gains near 1, the others offsets and biases of both signs.
All inputs are finite; a program needn't handle non-finite values.
Results may differ from a plain program's by a relative error of at most 0.011.
Values may be sent and summed in bfloat16 or wider, within the bound.
A program may use at most 192 MiB of HBM per device.

v0:
```python
import functools

import jax
import jax.numpy as jnp
import numpy as np
from jax import lax
from jax.experimental import pallas as pl
from jax.experimental.pallas import tpu as pltpu
from jax.sharding import PartitionSpec as P

HD = 64
D = 512
FF = 2048
SEG = 512
KLEN = 1024
OWN = 256
HEADS = 8
VOCAB = 256
MP = 8

EPSILON = 1e-05
MOMENTUM = 0.9
AVERAGE = 0.9
RATE = 0.3
PENALTY = 0.0001
WIDEN = 5.0
F32 = jnp.float32
BF16 = jnp.bfloat16
SCALE = HD ** (-0.5)


def dot_nn(a, b):
    return lax.dot_general(a, b, (((1,), (0,)), ((), ())), preferred_element_type=F32)


def dot_nt(a, b):
    return lax.dot_general(a, b, (((1,), (1,)), ((), ())), preferred_element_type=F32)


def smooth_unit(v):
    return 0.5 * v * (1.0 + jnp.tanh(0.7978845608028654 * (v + 0.044715 * v * v * v)))


def smooth_both(v):
    squared = v * v
    t = jnp.tanh(0.7978845608028654 * (v + 0.044715 * squared * v))
    half = 0.5 * (1.0 + t)
    slope = half + 0.5 * v * (1.0 - t * t) * (
        0.7978845608028654 * (1.0 + 3.0 * 0.044715 * squared)
    )
    return v * half, slope


def tables():
    freq = (1.0 / 10000.0 ** (np.arange(0, D, 2).astype(np.float32) / np.float32(D))).astype(
        np.float32
    )
    turned = []
    for half in range(2):
        distance = (SEG + half * OWN - np.arange(KLEN)) % KLEN
        angle = (distance.astype(np.float32)[:, None] * freq[None, :]).astype(np.float64)
        turned.append(np.concatenate([np.sin(angle), np.cos(angle)], axis=1).astype(np.float32))
    return jnp.asarray(np.stack(turned), BF16)


def norm_forward(values):
    centred = values - jnp.mean(values, axis=-1, keepdims=True)
    inverse = lax.rsqrt(jnp.mean(centred * centred, axis=-1, keepdims=True) + EPSILON)
    return centred * inverse, inverse


def norm_backward(grad, normed, inverse, gain):
    scaled = grad * gain
    grad_in = inverse * (
        scaled
        - jnp.mean(scaled, axis=-1, keepdims=True)
        - normed * jnp.mean(scaled * normed, axis=-1, keepdims=True)
    )
    return (
        grad_in,
        jnp.sum(grad * normed, axis=0, keepdims=True),
        jnp.sum(grad, axis=0, keepdims=True),
    )


def transposed(value):
    return value.astype(F32).T


ROWS = 64
VMEM_SPEC = pl.BlockSpec(memory_space=pltpu.VMEM)
VMEM_LIMIT = 60 * 1024 * 1024


ANY_SPEC = pl.BlockSpec(memory_space=pl.ANY)
MESH = pl.DeviceIdType.MESH

ATT, FFN, SMALL = 0, 1, 2
GROUPS = (
    (ATT, 0, (("z", 0, 3), ("x", 3, 5)), 16),
    (FFN, 0, (("z", 0, 1), ("x", 1, 2)), 128),
    (ATT, 1, (("z", 0, 2), ("x", 2, 5)), 16),
    (FFN, 1, (("z", 0, 1), ("x", 1, 2)), 128),
)
SUM_GROUPS = (
    (ATT, 0, (0, 4), (("z", 0, 2), ("x", 2, 4)), 16),
    (FFN, 0, (0, 2), (("z", 0, 1), ("x", 1, 2)), 128),
    (ATT, 1, (0, 4), (("z", 0, 2), ("x", 2, 4)), 16),
    (FFN, 1, (0, 2), (("z", 0, 1), ("x", 1, 2)), 128),
    (SMALL, 0, (0, 1), (("z", 0, 1),), 16),
    (ATT, 0, (4, 5), (("z", 0, 1),), 16),
    (ATT, 1, (4, 5), (("x", 0, 1),), 16),
)


class Place:
    def __init__(self):
        dp, mp = lax.axis_index("dp"), lax.axis_index("mp")
        self.x, self.z = dp // 4, dp % 4
        self.y, self.core = mp // 2, mp % 2

    def device(self, x=None, z=None, y=None, core=None):
        x = self.x if x is None else x
        z = self.z if z is None else z
        y = self.y if y is None else y
        core = self.core if core is None else core
        return {"dp": x * 4 + z, "mp": y * 2 + core}

    def along(self, axis, shift):
        return self.device(**{axis: (getattr(self, axis) + shift + 4) % 4})

    def sibling(self):
        return self.device(core=1 - self.core)

    def greet(self):
        partners = [self.along(axis, s) for axis in "xzy" for s in (1, 2, 3)] + [self.sibling()]
        barrier = pltpu.get_barrier_semaphore()
        for partner in partners:
            pl.semaphore_signal(barrier, inc=1, device_id=partner, device_id_type=MESH)

    def greeted(self):
        pl.semaphore_wait(pltpu.get_barrier_semaphore(), 10)


def send(source, target, sems, index, device):
    copy = pltpu.make_async_remote_copy(
        src_ref=source,
        dst_ref=target,
        send_sem=sems[0].at[index],
        recv_sem=sems[1].at[index],
        device_id=device,
        device_id_type=MESH,
    )
    copy.start()
    return copy


def spread_rank(rank, width):
    blocks = rank.shape[1]
    lane = lax.broadcasted_iota(jnp.int32, (blocks, width), 1) // (width // blocks)
    row = lax.broadcasted_iota(jnp.int32, (blocks, width), 0)
    return dot_nn(rank, jnp.where(lane == row, 1.0, 0.0))


class Weights:
    def __init__(self, here, sources, targets, sems, local_sem):
        self.here, self.sources, self.targets = here, sources, targets
        self.sems, self.local_sem = sems, local_sem
        self.copies = [[None] * len(GROUPS) for _ in range(3)]
        self.local = [None] * len(GROUPS)

    def slice_at(self, axis, rows):
        return pl.ds(pl.multiple_of(getattr(self.here, axis) * rows, rows), rows)

    def one(self, g):
        kind, layer, parts, rows = GROUPS[g]
        source, target = self.sources[kind].at[layer], self.targets[kind].at[layer]
        self.local[g] = pltpu.make_async_copy(source, target.at[:, 0, 0], self.local_sem.at[g])
        self.local[g].start()
        self.copies[0][g] = [
            send(
                source.at[low:high, self.slice_at(axis, rows)],
                target.at[low:high, 0, r, self.slice_at(axis, rows)],
                self.sems[0],
                g * 6 + p * 3 + r - 1,
                self.here.along("y", -r),
            )
            for p, (axis, low, high) in enumerate(parts)
            for r in (1, 2, 3)
        ]

    def two(self, g):
        kind, layer, parts, rows = GROUPS[g]
        target = self.targets[kind].at[layer]
        for copy in self.copies[0][g]:
            copy.wait_recv()
        self.copies[1][g] = []
        for p, (axis, low, high) in enumerate(parts):
            part = target.at[low:high, 0, 1:4, self.slice_at(axis, rows)]
            for s in (1, 2, 3):
                self.copies[1][g].append(
                    send(part, part, self.sems[1], g * 6 + p * 3 + s - 1, self.here.along(axis, s))
                )

    def three(self, g):
        kind, layer, _, _ = GROUPS[g]
        target = self.targets[kind].at[layer]
        for copy in self.copies[1][g]:
            copy.wait_recv()
        self.local[g].wait()
        self.copies[2][g] = [
            send(target.at[:, 0], target.at[:, 1], self.sems[2], g, self.here.sibling())
        ]

    def load(self, g, buffer, sem):
        kind, layer, _, _ = GROUPS[g]
        self.copies[2][g][0].wait_recv()
        copy = pltpu.make_async_copy(self.targets[kind].at[layer], buffer, sem)
        copy.start()
        return copy

    def end(self):
        for stage in self.copies:
            for copies in stage:
                for copy in copies:
                    copy.wait_send()


def forward_step(
    att_weight_ref,
    ff_weight_ref,
    att_rank_ref,
    ff_rank_ref,
    head_bias_ref,
    inner_bias_ref,
    embedding_ref,
    inputs_ref,
    targets_ref,
    valid_ref,
    memory_ref,
    norm_ref,
    table_hbm,
    att_out,
    ff_out,
    new_memory_ref,
    prob_out,
    bias_out,
    count_out,
    low_out,
    query_u_out,
    query_w_out,
    mixed_out,
    normed_one_out,
    inverse_one_out,
    normed_two_out,
    inverse_two_out,
    grad_ref,
    grad_embedding_ref,
    ce_ref,
    att_ref,
    ff_ref,
    bias_ref,
    count_ref,
    rank_ref,
    block_rank_ref,
    count_z,
    count_x,
    att_w,
    ff_w,
    memory_w,
    table_ref,
    turned_ref,
    embed_ref,
    keys_ref,
    values_ref,
    rel_ref,
    score_ref,
    prob_ref,
    low_prob_ref,
    part_ref,
    hidden_ref,
    first_send,
    first_recv,
    second_send,
    second_recv,
    third_send,
    third_recv,
    extra_send,
    extra_recv,
    local_sem,
    load_sem,
    prob_sem,
):
    here = Place()
    here.greet()
    extra = (extra_send, extra_recv)
    rank_ref[...] = spread_rank(att_rank_ref[...], D)
    block_rank_ref[...] = spread_rank(ff_rank_ref[...], 256)

    def mask_attention(layer):
        for i in range(5):
            kept = rank_ref[layer * 5 + i : layer * 5 + i + 1, :] < 1.5
            att_ref[layer, i] = jnp.where(kept, att_weight_ref[layer, i], 0.0).astype(BF16)

    def mask_feedforward(layer):
        for i in range(16):
            kept = block_rank_ref[layer * 16 + i : layer * 16 + i + 1, :] < 1.5
            rows = slice(i % 8 * 64, i % 8 * 64 + 64)
            ff_ref[layer, i // 8, rows, :] = jnp.where(
                kept, ff_weight_ref[layer, i // 8, rows, :], 0.0
            ).astype(BF16)

    mask_attention(0)
    here.greeted()
    weights = Weights(
        here,
        (att_ref, ff_ref),
        (att_out, ff_out),
        ((first_send, first_recv), (second_send, second_recv), (third_send, third_recv)),
        local_sem,
    )
    weights.one(0)
    mask_feedforward(0)
    weights.one(1)
    counted = jnp.sum(valid_ref[...].astype(F32), axis=1, keepdims=True)
    count_ref[...] = jnp.broadcast_to(jnp.sum(counted, axis=0, keepdims=True), (8, 128))
    bias_ref[6:8, :] = jnp.zeros((2, 128), F32)
    for l in range(2):
        bias_ref[3 * l : 3 * l + 1, :] = jnp.concatenate(
            [head_bias_ref[l, k : k + 1, :] for k in range(2)], axis=1
        )
        for k in range(2):
            bias_ref[3 * l + 1 + k : 3 * l + 2 + k, :] = inner_bias_ref[
                l : l + 1, k * 128 : (k + 1) * 128
            ]
    count_z[here.z] = count_ref[...]
    count_copies = [
        send(count_ref, count_z.at[here.z], extra, s - 1, here.along("z", s)) for s in (1, 2, 3)
    ]
    bias_copies = [
        send(bias_ref, bias_out.at[0, r], extra, 2 + r, here.along("y", -r)) for r in (1, 2, 3)
    ]
    bias_out[0, 0] = bias_ref[...]
    mask_attention(1)
    weights.one(2)
    mask_feedforward(1)
    weights.one(3)
    loads = [
        pltpu.make_async_copy(table_hbm.at[here.core], table_ref, load_sem.at[0]),
        pltpu.make_async_copy(memory_ref.at[0, here.y], memory_w.at[0], load_sem.at[1]),
        pltpu.make_async_copy(memory_ref.at[1, here.y], memory_w.at[1], load_sem.at[2]),
    ]
    for copy in loads:
        copy.start()

    own_rows = pl.ds(pl.multiple_of(here.core * OWN, OWN), OWN)
    turned_ref[...] = jnp.zeros_like(turned_ref)
    turned_ref[0:4, :] = inputs_ref[...].astype(F32)
    turned_ref[8:12, :] = targets_ref[...].astype(F32)
    turned_ref[16:20, :] = valid_ref[...].astype(F32)
    columns = turned_ref[...].T
    turned_ref[:, 0:128] = columns[0:128]
    turned_ref[:, 128:256] = columns[128:256]
    turned_ref[:, 256:384] = columns[256:384]
    turned_ref[:, 384:512] = columns[384:512]
    embedding = embedding_ref[...]
    embedding_low = embedding.astype(BF16)
    vocab_id = lax.broadcasted_iota(jnp.int32, (128, VOCAB), 1).astype(F32)

    def onehot(column):
        return jnp.where(column == vocab_id, 1.0, 0.0)

    for segment in range(4):
        for b in range(4):
            tokens = turned_ref[:, b * 128 + segment : b * 128 + segment + 1]
            embed_ref[segment, b * 128 : (b + 1) * 128, :] = dot_nn(
                onehot(tokens).astype(BF16), embedding_low
            ).astype(BF16)
    memory_zero = pltpu.make_async_copy(embed_ref, new_memory_ref.at[0], load_sem.at[3])
    memory_zero.start()
    weights.two(0)
    low_out[0] = embed_ref[here.y]
    rest_one = embedding - embedding_low.astype(F32)
    middle_part = rest_one.astype(BF16)
    rest_two = (rest_one - middle_part.astype(F32)).astype(BF16)
    lane = lax.broadcasted_iota(jnp.int32, (128, 128), 1)
    own_targets, own_valid = [], []
    for b in range(2):
        block = turned_ref[:, pl.ds(pl.multiple_of(here.core * 256 + b * 128, 128), 128)]

        def column(at):
            return jnp.sum(jnp.where(lane == here.y + at, block, 0.0), axis=1, keepdims=True)

        mine = onehot(column(0)).astype(BF16)
        hidden_ref[b * 128 : (b + 1) * 128, :] = (
            dot_nn(mine, embedding_low) + dot_nn(mine, middle_part)
        ) + dot_nn(mine, rest_two)
        own_targets.append(onehot(column(8)))
        own_valid.append(column(16))
    weights.three(0)
    for copy in bias_copies:
        copy.wait_recv()
    bias_last = send(bias_out.at[0], bias_out.at[1], extra, 6, here.sibling())
    for copy in count_copies:
        copy.wait_recv()
    count_x[here.x] = (count_z[0] + count_z[1]) + (count_z[2] + count_z[3])
    count_last = [
        send(count_x.at[here.x], count_x.at[here.x], extra, 6 + s, here.along("x", s))
        for s in (1, 2, 3)
    ]
    weights.two(1)
    for copy in loads:
        copy.wait()
    bias_last.wait_recv()
    pending = []
    offset = here.core * OWN
    lane_head = lax.broadcasted_iota(jnp.int32, (OWN, 256), 1) // HD

    def project(layer):
        own_low = hidden_ref[...].astype(BF16)
        query = dot_nt(own_low, att_w[layer, 0].reshape(D, D))
        for which, target in ((0, query_u_out), (1, query_w_out)):
            bias = jnp.concatenate(
                [
                    bias_out[cc, r, 3 * layer : 3 * layer + 1, which * HD : (which + 1) * HD]
                    for cc in range(2)
                    for r in range(4)
                ],
                axis=1,
            )
            target[layer] = (query + bias).astype(BF16)
        key_w, value_w = att_w[layer, 1].reshape(D, D), att_w[layer, 2].reshape(D, D)
        for half in range(2):
            rows = memory_w[layer] if half == 0 else low_out[layer]
            cols = slice(half * SEG, (half + 1) * SEG)
            keys_ref[:, cols] = dot_nt(key_w, rows).astype(BF16)
            values = dot_nt(rows, value_w).astype(BF16)
            values_ref[0, cols, :] = values[:, 0:256]
            values_ref[1, cols, :] = values[:, 256:512]
        rel_ref[...] = dot_nt(att_w[layer, 3].reshape(D, D), table_ref[...]).astype(BF16)
        part_ref[...] = jnp.zeros_like(part_ref)

    def head(layer):
        def run(h, carry):
            group = h // 4
            slot = h % 2
            mine = lane_head == h % 4
            lanes = pl.ds(pl.multiple_of(group * 256, 256), 256)
            query_u = jnp.where(mine, query_u_out[layer, :, lanes].astype(F32), 0.0).astype(BF16)
            query_w = jnp.where(mine, query_w_out[layer, :, lanes].astype(F32), 0.0).astype(BF16)
            score_ref[...] = dot_nn(query_w, rel_ref[lanes, :])

            @pl.when(h >= 2)
            def _():
                pltpu.make_async_copy(
                    prob_ref.at[slot], prob_out.at[layer, h], prob_sem.at[slot]
                ).wait()

            prob_ref[slot] = dot_nn(query_u, keys_ref[lanes, :])
            for b in range(0, OWN, ROWS):
                rows = slice(b, b + ROWS)
                moved = pltpu.roll(score_ref[rows, :], b, 1, stride=1, stride_axis=0)
                score = (prob_ref[slot, rows, :] + moved) * SCALE
                key_id = lax.broadcasted_iota(jnp.int32, (ROWS, KLEN), 1)
                query_id = lax.broadcasted_iota(jnp.int32, (ROWS, KLEN), 0) + (offset + b + SEG)
                score = jnp.where(key_id <= query_id, score, -1e30)
                expo = jnp.exp(score - jnp.max(score, axis=-1, keepdims=True))
                prob = expo * (1.0 / jnp.sum(expo, axis=-1, keepdims=True))
                prob_ref[slot, rows, :] = prob
                low_prob_ref[rows, :] = prob.astype(BF16)
            pltpu.make_async_copy(
                prob_ref.at[slot], prob_out.at[layer, h], prob_sem.at[slot]
            ).start()
            mixed = dot_nn(low_prob_ref[...], values_ref[group])
            part_ref[group] = part_ref[group] + jnp.where(mine, mixed, 0.0)
            return carry

        return run

    def attend(layer):
        for slot in range(2):
            pltpu.make_async_copy(
                prob_ref.at[slot], prob_out.at[layer, 6 + slot], prob_sem.at[slot]
            ).wait()
        mixed_out[layer, :, 0:256] = part_ref[0].astype(BF16)
        mixed_out[layer, :, 256:512] = part_ref[1].astype(BF16)
        attended = dot_nn(mixed_out[layer], att_w[layer, 4].reshape(D, D))
        normed_one, inverse_one = norm_forward(hidden_ref[...] + attended)
        normed_one_out[layer] = normed_one
        inverse_one_out[layer] = inverse_one
        return normed_one * norm_ref[0, layer : layer + 1, :] + norm_ref[1, layer : layer + 1, :]

    def feed(layer, middle):
        middle_low = middle.astype(BF16)
        branch = jnp.zeros((OWN, D), F32)
        for cc in range(2):
            for r in range(4):
                bias = jnp.concatenate(
                    [bias_out[cc, r, 3 * layer + 1 + i : 3 * layer + 2 + i, :] for i in range(2)],
                    axis=1,
                )
                inner = dot_nn(middle_low, ff_w[layer, 0, cc, r]) + bias
                branch = branch + dot_nt(smooth_unit(inner).astype(BF16), ff_w[layer, 1, cc, r])
        normed_two, inverse_two = norm_forward(middle + (branch + norm_ref[4, layer : layer + 1, :]))
        normed_two_out[layer] = normed_two
        inverse_two_out[layer] = inverse_two
        hidden_ref[...] = normed_two * norm_ref[2, layer : layer + 1, :] + norm_ref[3, layer : layer + 1, :]

    weights.load(0, att_w.at[0], load_sem.at[4]).wait()
    project(0)
    weights.two(2)
    lax.fori_loop(0, 4, head(0), 0)
    weights.three(1)
    weights.two(3)
    lax.fori_loop(4, 8, head(0), 0)
    weights.three(2)
    feed_load = weights.load(1, ff_w.at[0], load_sem.at[5])
    middle = attend(0)
    feed_load.wait()
    feed(0, middle)
    low_out[1, own_rows, :] = hidden_ref[...].astype(BF16)
    own_low = low_out.at[1, own_rows]
    swap = send(own_low, own_low, extra, 10, here.sibling())
    spread_at = new_memory_ref.at[1, here.y, own_rows]
    spread = [send(own_low, spread_at, extra, 10 + s, here.along("y", s)) for s in (1, 2, 3)]
    spread_own = pltpu.make_async_copy(own_low, spread_at, load_sem.at[6])
    spread_own.start()
    attention_one = weights.load(2, att_w.at[1], load_sem.at[7])
    swap.wait_recv()
    attention_one.wait()
    project(1)
    lax.fori_loop(0, 4, head(1), 0)
    weights.three(3)
    for copy in spread:
        copy.wait_recv()
    spread_own.wait()
    spread_all = new_memory_ref.at[1, :, own_rows]
    spread_last = send(spread_all, spread_all, extra, 14, here.sibling())
    lax.fori_loop(4, 8, head(1), 0)
    feed_load = weights.load(3, ff_w.at[1], load_sem.at[5])
    middle = attend(1)
    feed_load.wait()
    feed(1, middle)
    for copy in count_last:
        copy.wait_recv()
    count_all = (count_x[0] + count_x[1]) + (count_x[2] + count_x[3])
    count_out[...] = count_all

    final_low = hidden_ref[...].astype(BF16)
    logit_scale = D ** (-0.5)
    logits = dot_nt(final_low, embedding_low) * logit_scale
    picked = jnp.concatenate(own_targets, axis=0)
    valid = jnp.concatenate(own_valid, axis=0)
    peak = jnp.max(logits, axis=-1, keepdims=True)
    log_total = peak + jnp.log(jnp.sum(jnp.exp(logits - peak), axis=-1, keepdims=True))
    losses = valid * (log_total - jnp.sum(logits * picked, axis=-1, keepdims=True))
    ce_ref[...] = jnp.broadcast_to(jnp.sum(losses, axis=0, keepdims=True), (8, 128))
    grad_logits = (valid * (jnp.exp(logits - log_total) - picked) / count_all[0:1, 0:1]).astype(
        BF16
    )
    grad_ref[...] = dot_nn(grad_logits, embedding_low) * logit_scale
    grad_embedding_ref[...] = (
        dot_nn(transposed(grad_logits).astype(BF16), final_low) * logit_scale
    ).reshape(MP, 32, D)
    memory_zero.wait()
    spread_last.wait()
    for copy in count_copies + bias_copies + [bias_last] + count_last + [swap] + spread:
        copy.wait_send()
    weights.end()


def forward_all(*operands):
    vmem, hbm = VMEM_SPEC, ANY_SPEC
    outs = [
        (hbm, (2, 5, 2, 4, HD, D), BF16),
        (hbm, (2, 2, 2, 4, D, 256), BF16),
        (hbm, (2, 4, SEG, D), BF16),
        (hbm, (2, HEADS, OWN, KLEN), F32),
        (vmem, (2, 4, 8, 128), F32),
        (vmem, (8, 128), F32),
        (vmem, (2, SEG, D), BF16),
        (vmem, (2, OWN, D), BF16),
        (vmem, (2, OWN, D), BF16),
        (vmem, (2, OWN, D), BF16),
        (vmem, (2, OWN, D), F32),
        (vmem, (2, OWN, 1), F32),
        (vmem, (2, OWN, D), F32),
        (vmem, (2, OWN, 1), F32),
        (vmem, (OWN, D), F32),
        (vmem, (MP, 32, D), F32),
        (vmem, (8, 128), F32),
    ]
    return pl.pallas_call(
        forward_step,
        out_shape=[jax.ShapeDtypeStruct(s, t) for _, s, t in outs],
        in_specs=[vmem] * 10 + [hbm, vmem, hbm],
        out_specs=[m for m, _, _ in outs],
        scratch_shapes=[
            pltpu.VMEM((2, 5, HD, D), BF16),
            pltpu.VMEM((2, 2, D, 256), BF16),
            pltpu.VMEM((8, 128), F32),
            pltpu.VMEM((8, 128), F32),
            pltpu.VMEM((10, D), F32),
            pltpu.VMEM((32, 256), F32),
            pltpu.VMEM((4, 8, 128), F32),
            pltpu.VMEM((4, 8, 128), F32),
            pltpu.VMEM((2, 5, 2, 4, HD, D), BF16),
            pltpu.VMEM((2, 2, 2, 4, D, 256), BF16),
            pltpu.VMEM((2, SEG, D), BF16),
            pltpu.VMEM((KLEN, D), BF16),
            pltpu.VMEM((128, SEG), F32),
            pltpu.VMEM((4, SEG, D), BF16),
            pltpu.VMEM((D, KLEN), BF16),
            pltpu.VMEM((2, KLEN, 256), BF16),
            pltpu.VMEM((D, KLEN), BF16),
            pltpu.VMEM((OWN, KLEN), F32),
            pltpu.VMEM((2, OWN, KLEN), F32),
            pltpu.VMEM((OWN, KLEN), BF16),
            pltpu.VMEM((2, OWN, 256), F32),
            pltpu.VMEM((OWN, D), F32),
            pltpu.SemaphoreType.DMA((24,)),
            pltpu.SemaphoreType.DMA((24,)),
            pltpu.SemaphoreType.DMA((24,)),
            pltpu.SemaphoreType.DMA((24,)),
            pltpu.SemaphoreType.DMA((4,)),
            pltpu.SemaphoreType.DMA((4,)),
            pltpu.SemaphoreType.DMA((15,)),
            pltpu.SemaphoreType.DMA((15,)),
            pltpu.SemaphoreType.DMA((4,)),
            pltpu.SemaphoreType.DMA((8,)),
            pltpu.SemaphoreType.DMA((2,)),
        ],
        compiler_params=pltpu.CompilerParams(
            collective_id=0, has_side_effects=True, vmem_limit_bytes=VMEM_LIMIT
        ),
        name="forward_all",
    )(*operands)


SHAPES = {ATT: (HD, D), FFN: (D, 256), SMALL: (64, D)}


class Sums:
    def __init__(self, here, arrays, outs, buffers, sems):
        self.here, self.arrays, self.outs = here, arrays, outs
        self.pairs, self.ones, self.twos, self.threes = buffers
        self.sems = sems
        self.copies = [[[] for _ in SUM_GROUPS] for _ in range(5)]

    def slice_at(self, index, rows):
        return pl.ds(pl.multiple_of(index * rows, rows), rows)

    def arrived(self, stage, g):
        for copy in self.copies[stage][g]:
            copy.wait_recv()

    def pair(self, g):
        kind, layer, (base, end), _, _ = SUM_GROUPS[g]
        self.copies[0][g].append(
            send(
                self.arrays[kind].at[layer, base:end, 1],
                self.pairs[g],
                self.sems[0],
                g,
                self.here.sibling(),
            )
        )

    def one(self, g):
        kind, layer, (base, _), parts, rows = SUM_GROUPS[g]
        self.arrived(0, g)
        pair = self.pairs[g]
        for m in range(pair.shape[0]):
            for r in range(4):
                pair[m, r] = (
                    pair[m, r].astype(F32) + self.arrays[kind][layer, base + m, 0, r].astype(F32)
                ).astype(BF16)
        for p, (axis, low, high) in enumerate(parts):
            for s in (1, 2, 3):
                goal = (getattr(self.here, axis) + s) % 4
                self.copies[1][g].append(
                    send(
                        pair.at[low:high, :, self.slice_at(goal, rows)],
                        self.ones[g][p].at[s - 1],
                        self.sems[1],
                        g * 6 + p * 3 + s - 1,
                        self.here.along(axis, s),
                    )
                )

    def two(self, g):
        kind, layer, (base, _), parts, rows = SUM_GROUPS[g]
        self.arrived(1, g)
        for p, (axis, low, high) in enumerate(parts):
            got = self.ones[g][p]
            own = self.pairs[g].at[low:high, :, self.slice_at(getattr(self.here, axis), rows)]
            for m in range(high - low):
                for r in range(4):
                    got[0, m, r] = (
                        (own[m, r].astype(F32) + got[0, m, r].astype(F32))
                        + (got[1, m, r].astype(F32) + got[2, m, r].astype(F32))
                    ).astype(BF16)
            for r in (1, 2, 3):
                self.copies[2][g].append(
                    send(
                        got.at[0, :, r],
                        self.twos[g][p].at[r - 1],
                        self.sems[2],
                        g * 6 + p * 3 + r - 1,
                        self.here.along("y", r),
                    )
                )

    def three(self, g):
        kind, layer, (base, _), parts, rows = SUM_GROUPS[g]
        self.arrived(2, g)
        for p, (axis, low, high) in enumerate(parts):
            other = "x" if axis == "z" else "z"
            got, every = self.twos[g][p], self.threes[g][p]
            index = getattr(self.here, other)
            for m in range(high - low):
                every[index, m] = (
                    (self.ones[g][p][0, m, 0].astype(F32) + got[0, m].astype(F32))
                    + (got[1, m].astype(F32) + got[2, m].astype(F32))
                ).astype(BF16)
            for s in (1, 2, 3):
                self.copies[3][g].append(
                    send(
                        every.at[index],
                        every.at[index],
                        self.sems[3],
                        g * 6 + p * 3 + s - 1,
                        self.here.along(other, s),
                    )
                )

    def four(self, g):
        kind, layer, (base, _), parts, rows = SUM_GROUPS[g]
        self.arrived(3, g)
        for p, (axis, low, high) in enumerate(parts):
            every = self.threes[g][p]
            part = self.slice_at(getattr(self.here, axis), rows)
            for m in range(high - low):
                self.outs[kind][layer, base + low + m, part] = (
                    (every[0, m].astype(F32) + every[1, m].astype(F32))
                    + (every[2, m].astype(F32) + every[3, m].astype(F32))
                ).astype(BF16)
            target = self.outs[kind].at[layer, base + low : base + high, part]
            for s in (1, 2, 3):
                self.copies[4][g].append(
                    send(
                        target,
                        target,
                        self.sems[4],
                        g * 6 + p * 3 + s - 1,
                        self.here.along(axis, s),
                    )
                )

    def end(self):
        for stage in self.copies:
            for copies in stage:
                for copy in copies:
                    copy.wait_send()


def backward_step(
    att_hbm,
    ff_hbm,
    prob_hbm,
    memory_hbm,
    table_hbm,
    grad_hbm,
    grad_embedding_hbm,
    normed_two_hbm,
    bias_ref,
    norm_ref,
    inputs_ref,
    ce_ref,
    low_ref,
    query_u_ref,
    query_w_ref,
    mixed_ref,
    normed_one_ref,
    inverse_one_ref,
    inverse_two_ref,
    att_out,
    ff_out,
    small_out,
    ce_out,
    att_w,
    ff_w,
    memory_w,
    table_ref,
    prob_ref,
    grad_att_ref,
    grad_ff_ref,
    grad_small_ref,
    grad_ref,
    keys_ref,
    values_ref,
    rel_ref,
    gmix_ref,
    gmix_t_ref,
    query_t_ref,
    flip_t_ref,
    prob_grad_ref,
    score_grad_ref,
    low_prob_ref,
    flipped_ref,
    gquery_ref,
    gmemory_ref,
    ghidden_ref,
    got_ref,
    grel_ref,
    grad_bias_ref,
    grad_inner_ref,
    grad_norm_ref,
    ranked_ref,
    block_ref,
    ce_pair,
    ce_z,
    ce_y,
    ce_x,
    small_own,
    *scratch,
):
    here = Place()
    scratch = list(scratch)
    pairs = [scratch.pop(0) for _ in SUM_GROUPS]
    ones, twos, threes = [], [], []
    for group in SUM_GROUPS:
        for buffers in (ones, twos, threes):
            buffers.append([scratch.pop(0) for _ in group[3]])
    sems = [(scratch.pop(0), scratch.pop(0)) for _ in range(6)]
    load_sem, prob_sem = scratch
    extra = sems[5]
    sums = Sums(
        here,
        (grad_att_ref, grad_ff_ref, grad_small_ref),
        (att_out, ff_out, small_own),
        (pairs, ones, twos, threes),
        sems,
    )
    load_ff = pltpu.make_async_copy(ff_hbm.at[1], ff_w, load_sem.at[0])
    load_att = pltpu.make_async_copy(att_hbm.at[1], att_w, load_sem.at[1])
    loads = [
        pltpu.make_async_copy(memory_hbm.at[0, here.y], memory_w.at[0], load_sem.at[2]),
        pltpu.make_async_copy(memory_hbm.at[1, here.y], memory_w.at[1], load_sem.at[3]),
        pltpu.make_async_copy(table_hbm.at[here.core], table_ref, load_sem.at[4]),
        pltpu.make_async_copy(grad_embedding_hbm, ranked_ref, load_sem.at[5]),
    ]
    load_grad = pltpu.make_async_copy(grad_hbm, grad_ref, load_sem.at[6])
    load_grad.start()
    load_normed = pltpu.make_async_copy(
        normed_two_hbm.at[1], prob_grad_ref.at[:, 0:D], load_sem.at[7]
    )
    load_normed.start()
    load_ff.start()
    load_att.start()
    for copy in loads:
        copy.start()
    here.greet()
    here.greeted()
    own_rows = pl.ds(pl.multiple_of(here.core * OWN, OWN), OWN)
    their_rows = pl.ds(pl.multiple_of(OWN - here.core * OWN, OWN), OWN)
    ce_pair[here.core] = ce_ref[...]
    ce_copies = [send(ce_ref, ce_pair.at[here.core], extra, 0, here.sibling())]
    flip = (
        lax.broadcasted_iota(jnp.int32, (OWN, OWN), 0)
        + lax.broadcasted_iota(jnp.int32, (OWN, OWN), 1)
        == OWN - 1
    )
    flip = jnp.where(flip, 1.0, 0.0).astype(BF16)
    lane_head = lax.broadcasted_iota(jnp.int32, (OWN, 256), 1) // HD
    load_grad.wait()

    def spread_ce(step):
        source, target, axis, base = (
            (ce_pair, ce_z, "z", 1),
            (ce_z, ce_y, "y", 4),
            (ce_y, ce_x, "x", 7),
        )[step]
        for copy in ce_copies[-1:] if step == 0 else ce_copies[-3:]:
            copy.wait_recv()
        total = source[0] + source[1]
        if step:
            total = total + (source[2] + source[3])
        index = getattr(here, axis)
        target[index] = total
        for s in (1, 2, 3):
            ce_copies.append(
                send(target.at[index], target.at[index], extra, base + s - 1, here.along(axis, s))
            )

    def feed(layer):
        load_normed.wait()
        gsum, ggain, goffset = norm_backward(
            grad_ref[...], prob_grad_ref[:, 0:D], inverse_two_ref[layer], norm_ref[2, layer : layer + 1, :]
        )
        middle = normed_one_ref[layer] * norm_ref[0, layer : layer + 1, :] + norm_ref[1, layer : layer + 1, :]
        middle_low = middle.astype(BF16)
        middle_t = transposed(middle_low).astype(BF16)
        gbranch = gsum.astype(BF16)
        gbranch_t = transposed(gbranch).astype(BF16)
        gmiddle = gsum
        load_ff.wait()
        for cc in (1, 0):
            if cc == 0:
                sums.pair(1 if layer == 0 else 3)
            for r in range(4):
                bias = jnp.concatenate(
                    [bias_ref[cc, r, 3 * layer + 1 + i : 3 * layer + 2 + i, :] for i in range(2)],
                    axis=1,
                )
                inner = dot_nn(middle_low, ff_w[0, cc, r]) + bias
                active, slope = smooth_both(inner)
                ginner = (dot_nn(gbranch, ff_w[1, cc, r]) * slope).astype(BF16)
                grad_ff_ref[layer, 0, cc, r] = dot_nn(middle_t, ginner).astype(BF16)
                grad_ff_ref[layer, 1, cc, r] = dot_nn(gbranch_t, active.astype(BF16)).astype(BF16)
                grad_inner_ref[layer, cc, r] = jnp.sum(
                    ginner.astype(F32), axis=0, keepdims=True
                )
                gmiddle = gmiddle + dot_nt(ginner, ff_w[0, cc, r])
        rows = [jnp.sum(gsum, axis=0, keepdims=True)]
        gsum, ggain_one, goffset_one = norm_backward(
            gmiddle, normed_one_ref[layer], inverse_one_ref[layer], norm_ref[0, layer : layer + 1, :]
        )
        rows = [ggain_one, goffset_one, ggain, goffset] + rows
        for i, row in enumerate(rows):
            at = 8 * layer + i
            grad_norm_ref[at // 2, at % 2 : at % 2 + 1, :] = row
        grad_ref[...] = gsum

    def prepare(layer):
        gattended = grad_ref[...].astype(BF16)
        wide = dot_nn(transposed(mixed_ref[layer]).astype(BF16), gattended).astype(BF16)
        grad_att_ref[layer, 4] = wide.reshape(2, 4, HD, D)
        sums.pair(5 + layer)
        load_att.wait()
        gmix = dot_nt(gattended, att_w[4].reshape(D, D))
        gmix_ref[...] = gmix.astype(BF16)
        gmix_t_ref[...] = gmix.T.astype(BF16)
        query_t_ref[...] = transposed(query_u_ref[layer]).astype(BF16)
        flip_t_ref[...] = dot_nn(transposed(query_w_ref[layer]).astype(BF16), flip).astype(BF16)
        key_w, value_w = att_w[1].reshape(D, D), att_w[2].reshape(D, D)
        for half in range(2):
            rows = memory_w[layer] if half == 0 else low_ref[layer]
            cols = slice(half * SEG, (half + 1) * SEG)
            values_ref[:, cols] = dot_nt(value_w, rows).astype(BF16)
            keys = dot_nt(rows, key_w).astype(BF16)
            keys_ref[0, cols, :] = keys[:, 0:256]
            keys_ref[1, cols, :] = keys[:, 256:512]
        rel = dot_nt(table_ref[...], att_w[3].reshape(D, D)).astype(BF16)
        rel_ref[0] = rel[:, 0:256]
        rel_ref[1] = rel[:, 256:512]
        gquery_ref[...] = jnp.zeros_like(gquery_ref)

    def fetch(layer, n, slot):
        h = (n + 4) % HEADS
        return pltpu.make_async_copy(prob_hbm.at[layer, h], prob_ref.at[slot], prob_sem.at[slot])

    def head(layer):
        def run(n, carry):
            h = (n + 4) % HEADS
            group = h // 4
            slot = n % 2
            mine = lane_head == h % 4
            lanes = pl.ds(pl.multiple_of(group * 256, 256), 256)
            row = pl.ds(pl.multiple_of(h * HD, HD), HD)
            gmix_h = jnp.where(mine, gmix_ref[:, lanes].astype(F32), 0.0).astype(BF16)
            prob_grad_ref[...] = dot_nn(gmix_h, values_ref[lanes, :])
            fetch(layer, n, slot).wait()
            for b in range(0, OWN, ROWS):
                rows = slice(b, b + ROWS)
                prob = prob_ref[slot, rows, :]
                gprob = prob_grad_ref[rows, :]
                inner = jnp.sum(prob * gprob, axis=-1, keepdims=True)
                score_grad_ref[rows, :] = (prob * (gprob - inner)).astype(BF16)
                low_prob_ref[rows, :] = prob.astype(BF16)

            @pl.when(n < HEADS - 2)
            def _():
                fetch(layer, n + 2, slot).start()

            if layer == 1:
                @pl.when(n >= HEADS - 2)
                def _():
                    fetch(0, n + 2 - HEADS, slot).start()

            sgrad = score_grad_ref[...]
            gquery_ref[0, group] = gquery_ref[0, group] + jnp.where(
                mine, dot_nn(sgrad, keys_ref[group]), 0.0
            )
            gkey = dot_nn(query_t_ref[row, :], sgrad) * SCALE
            gvalue = dot_nn(gmix_t_ref[row, :], low_prob_ref[...])
            gmemory_ref[0, row, :] = gkey[:, 0:SEG].astype(BF16)
            gmemory_ref[1, row, :] = gvalue[:, 0:SEG].astype(BF16)
            ghidden_ref[0, row, :] = gkey[:, SEG:]
            ghidden_ref[1, row, :] = gvalue[:, SEG:]
            flipped = dot_nn(flip, sgrad).astype(BF16)
            flipped_ref[...] = pltpu.roll(flipped, KLEN - OWN + 1, 1, stride=1, stride_axis=0)
            gquery_ref[1, group] = gquery_ref[1, group] + jnp.where(
                mine, dot_nn(flipped_ref[...], rel_ref[group]), 0.0
            )
            grel_ref[row, :] = (dot_nn(flip_t_ref[row, :], flipped_ref[...]) * SCALE).astype(BF16)
            return carry

        return run

    def swap(layer, i):
        return send(
            ghidden_ref.at[:, 256 * i : 256 * i + 256, their_rows],
            got_ref.at[:, 256 - 256 * i : 512 - 256 * i],
            extra,
            10 + 2 * layer + i,
            here.sibling(),
        )

    def half(layer, group):
        own_low = low_ref[layer, own_rows, :]
        lanes = slice(group * 256, (group + 1) * 256)
        gquery_u = (gquery_ref[0, group] * SCALE).astype(BF16)
        gquery_w = dot_nn(flip, (gquery_ref[1, group] * SCALE).astype(BF16))
        grad_bias_ref[layer, 0:1, lanes] = jnp.sum(gquery_u.astype(F32), axis=0, keepdims=True)
        grad_bias_ref[layer, 1:2, lanes] = jnp.sum(gquery_w, axis=0, keepdims=True)
        gquery = gquery_u.astype(F32) + gquery_w
        grad_att_ref[layer, 0, group] = (
            dot_nn(gquery.T.astype(BF16), own_low).astype(BF16).reshape(4, HD, D)
        )
        grad_att_ref[layer, 3, group] = (
            dot_nn(grel_ref[lanes, :], table_ref[...]).astype(BF16).reshape(4, HD, D)
        )
        for i in range(2):
            part = dot_nn(gmemory_ref[i, lanes, :], memory_w[layer]) + dot_nn(
                ghidden_ref[i, lanes, :].astype(BF16), low_ref[layer]
            )
            grad_att_ref[layer, 1 + i, group] = part.astype(BF16).reshape(4, HD, D)
        return dot_nn(gquery.astype(BF16), att_w[0, group].reshape(256, D))

    def finish(swaps):
        for copy in swaps:
            copy.wait_recv()
        for i in range(2):
            total = (ghidden_ref[i, :, own_rows] + got_ref[i]).astype(BF16)
            grad_ref[...] += dot_nn(transposed(total).astype(BF16), att_w[1 + i].reshape(D, D))

    fetch(1, 0, 0).start()
    fetch(1, 1, 1).start()
    feed(1)
    load_ff = pltpu.make_async_copy(ff_hbm.at[0], ff_w, load_sem.at[0])
    load_ff.start()
    spread_ce(0)
    for copy in loads:
        copy.wait()
    prepare(1)
    sums.one(3)
    sums.one(6)
    lax.fori_loop(0, 4, head(1), 0)
    swaps_one = [swap(1, 1)]
    grad_ref[...] += half(1, 1)
    sums.pair(2)
    lax.fori_loop(4, HEADS, head(1), 0)
    swaps_one.append(swap(1, 0))
    load_normed = pltpu.make_async_copy(
        normed_two_hbm.at[0], prob_grad_ref.at[:, 0:D], load_sem.at[7]
    )
    load_normed.start()
    spread_ce(1)
    grad_ref[...] += half(1, 0)
    sums.one(2)
    sums.two(3)
    sums.two(6)
    finish(swaps_one)
    load_att = pltpu.make_async_copy(att_hbm.at[0], att_w, load_sem.at[1])
    load_att.start()
    feed(0)
    spread_ce(2)
    for copy in swaps_one:
        copy.wait_send()
    prepare(0)
    sums.one(1)
    sums.one(5)
    sums.two(2)
    lax.fori_loop(0, 4, head(0), 0)
    swaps_zero = [swap(0, 1)]
    grad_ref[...] += half(0, 1)
    sums.pair(0)
    sums.three(3)
    sums.three(6)
    lax.fori_loop(4, HEADS, head(0), 0)
    swaps_zero.append(swap(0, 0))
    grad_ref[...] += half(0, 0)
    sums.one(0)
    sums.two(1)
    sums.two(5)
    sums.three(2)
    finish(swaps_zero)

    tokens = inputs_ref[pl.ds(here.y, 1), own_rows]
    onehot = jnp.where(
        tokens == lax.broadcasted_iota(jnp.int32, (VOCAB, OWN), 0), 1.0, 0.0
    ).astype(BF16)
    grad = grad_ref[...]
    high = grad.astype(BF16)
    rest = (grad - high.astype(F32)).astype(BF16)
    ranked_ref[...] += (dot_nn(onehot, high) + dot_nn(onehot, rest)).reshape(MP, 32, D)
    block_ref[...] = jnp.zeros_like(block_ref)
    for cc in range(2):
        for r in range(4):
            device = ((here.y + r) % 4) * 2 + (here.core + cc) % 2
            first = (cc * 4 + r) * HD
            block_ref[0:32, :] = ranked_ref[device]
            block_ref[32:34, :] = grad_norm_ref[device]
            block_ref[34:35, 0:256] = jnp.concatenate(
                [
                    grad_bias_ref[l, k : k + 1, first : first + HD]
                    for l in range(2)
                    for k in range(2)
                ],
                axis=1,
            )
            block_ref[35:36, :] = jnp.concatenate(
                [grad_inner_ref[l, cc, r] for l in range(2)], axis=1
            )
            grad_small_ref[0, 0, cc, r] = block_ref[...].astype(BF16)
    sums.pair(4)
    sums.four(3)
    sums.four(6)
    sums.one(4)
    sums.two(0)
    sums.three(1)
    sums.three(5)
    sums.two(4)
    sums.four(2)
    sums.three(0)
    sums.three(4)
    sums.four(1)
    sums.four(5)
    for copy in ce_copies[-3:]:
        copy.wait_recv()
    ce_out[...] = (ce_x[0] + ce_x[1]) + (ce_x[2] + ce_x[3])
    sums.four(4)
    sums.four(0)
    sums.arrived(4, 4)
    small_out[here.y, here.core] = small_own[0, 0]
    piece = small_out.at[here.y, here.core]
    small_copies = [send(piece, piece, extra, 13 + r, here.along("y", r)) for r in (1, 2, 3)]
    for copy in small_copies:
        copy.wait_recv()
    piece = small_out.at[:, here.core]
    last = send(piece, piece, extra, 17, here.sibling())
    for g in (3, 6, 2, 1, 5, 0):
        sums.arrived(4, g)
    last.wait()
    for copy in ce_copies + swaps_zero + small_copies:
        copy.wait_send()
    sums.end()


def backward_all(*operands):
    vmem, hbm = VMEM_SPEC, ANY_SPEC
    outs = [
        ((2, 5, HD, D), BF16),
        ((2, 2, D, 256), BF16),
        ((4, 2, 64, D), BF16),
        ((8, 128), F32),
    ]
    scratch = [
        pltpu.VMEM((5, 2, 4, HD, D), BF16),
        pltpu.VMEM((2, 2, 4, D, 256), BF16),
        pltpu.VMEM((2, SEG, D), BF16),
        pltpu.VMEM((KLEN, D), BF16),
        pltpu.VMEM((2, OWN, KLEN), F32),
        pltpu.VMEM((2, 5, 2, 4, HD, D), BF16),
        pltpu.VMEM((2, 2, 2, 4, D, 256), BF16),
        pltpu.VMEM((1, 1, 2, 4, 64, D), BF16),
        pltpu.VMEM((OWN, D), F32),
        pltpu.VMEM((2, KLEN, 256), BF16),
        pltpu.VMEM((D, KLEN), BF16),
        pltpu.VMEM((2, KLEN, 256), BF16),
        pltpu.VMEM((OWN, D), BF16),
        pltpu.VMEM((D, OWN), BF16),
        pltpu.VMEM((D, OWN), BF16),
        pltpu.VMEM((D, OWN), BF16),
        pltpu.VMEM((OWN, KLEN), F32),
        pltpu.VMEM((OWN, KLEN), BF16),
        pltpu.VMEM((OWN, KLEN), BF16),
        pltpu.VMEM((OWN, KLEN), BF16),
        pltpu.VMEM((2, 2, OWN, 256), F32),
        pltpu.VMEM((2, D, SEG), BF16),
        pltpu.VMEM((2, D, SEG), F32),
        pltpu.VMEM((2, D, OWN), F32),
        pltpu.VMEM((D, KLEN), BF16),
        pltpu.VMEM((2, 2, D), F32),
        pltpu.VMEM((2, 2, 4, 1, 256), F32),
        pltpu.VMEM((MP, 2, D), F32),
        pltpu.VMEM((MP, 32, D), F32),
        pltpu.VMEM((64, D), F32),
        pltpu.VMEM((2, 8, 128), F32),
        pltpu.VMEM((4, 8, 128), F32),
        pltpu.VMEM((4, 8, 128), F32),
        pltpu.VMEM((4, 8, 128), F32),
        pltpu.VMEM((1, 1, 64, D), BF16),
    ]
    scratch += [pltpu.VMEM((hi - lo, 4) + SHAPES[k], BF16) for k, _, (lo, hi), _, _ in SUM_GROUPS]
    for kind, _, _, parts, rows in SUM_GROUPS:
        width = SHAPES[kind][1]
        scratch += [pltpu.VMEM((3, hi - lo, 4, rows, width), BF16) for _, lo, hi in parts]
        scratch += [pltpu.VMEM((3, hi - lo, rows, width), BF16) for _, lo, hi in parts]
        scratch += [pltpu.VMEM((4, hi - lo, rows, width), BF16) for _, lo, hi in parts]
    for n in (7, 42, 42, 42, 42, 18):
        scratch += [pltpu.SemaphoreType.DMA((n,)), pltpu.SemaphoreType.DMA((n,))]
    scratch += [pltpu.SemaphoreType.DMA((8,)), pltpu.SemaphoreType.DMA((2,))]
    return pl.pallas_call(
        backward_step,
        out_shape=[jax.ShapeDtypeStruct(s, t) for s, t in outs],
        in_specs=[hbm] * 8 + [vmem] * 11,
        out_specs=[vmem] * 4,
        scratch_shapes=scratch,
        compiler_params=pltpu.CompilerParams(
            collective_id=1, has_side_effects=True, vmem_limit_bytes=63 * 1024 * 1024
        ),
        name="backward_all",
    )(*operands)


def advance_one(grad, weight, moment):
    moment_next = MOMENTUM * moment + grad
    return moment_next, grad + MOMENTUM * moment_next


def masked(grad, weight, rank):
    coefficient = jnp.where(rank < 1.5, 1.0, jnp.where(rank < 2.5, WIDEN, 0.0))
    return jnp.where(rank < 2.5, grad, 0.0) + (2.0 * PENALTY) * weight * coefficient


def square_sum(value):
    return jnp.sum(value * value, axis=0, keepdims=True)


def moments_kernel(
    att_w_hbm,
    att_m_hbm,
    ff_w_hbm,
    ff_m_hbm,
    new_memory_hbm,
    att_sum_ref,
    ff_sum_ref,
    small_ref,
    att_rank_ref,
    ff_rank_ref,
    embedding_m_ref,
    head_w_ref,
    head_m_ref,
    inner_w_ref,
    inner_m_ref,
    norm_m_ref,
    att_g_hbm,
    att_m_out,
    ff_g_hbm,
    ff_m_out,
    new_memory_out,
    embedding_g_ref,
    embedding_m_out,
    head_g_ref,
    head_m_out,
    inner_g_ref,
    inner_m_out,
    norm_g_ref,
    norm_m_out,
    part_ref,
    att_w,
    att_m,
    att_g,
    ff_w,
    ff_m,
    ff_g,
    att_rank,
    ff_rank,
    memory_ref,
    load_sem,
    store_sem,
    memory_sem,
):
    loads, stores = [], []
    for l in range(2):
        for i, (source, target) in enumerate(
            ((ff_w_hbm, ff_w), (ff_m_hbm, ff_m), (att_w_hbm, att_w), (att_m_hbm, att_m))
        ):
            copy = pltpu.make_async_copy(source.at[l], target.at[l], load_sem.at[4 * l + i])
            copy.start()
            loads.append(copy)
    memory_in = pltpu.make_async_copy(new_memory_hbm, memory_ref, memory_sem.at[0])
    memory_in.start()
    att_rank[...] = spread_rank(att_rank_ref[...], D)
    ff_rank[...] = spread_rank(ff_rank_ref[...], 256)

    small = small_ref[lax.axis_index("mp") // 2, lax.axis_index("mp") % 2].astype(F32)
    head_sums = [jnp.zeros((1, HD), F32)] * 2
    inner_sums = [jnp.zeros((1, 256), F32)] * 2
    for l in range(2):
        for k in range(2):
            at = (l * 2 + k) * HD
            grad = small[34:35, at : at + HD]
            head_g_ref[l, k : k + 1, :] = grad
            weight = head_w_ref[l, k : k + 1, :]
            moment, direction = advance_one(grad, weight, head_m_ref[l, k : k + 1, :])
            head_m_out[l, k : k + 1, :] = moment
            head_sums[0] = head_sums[0] + weight * weight
            head_sums[1] = head_sums[1] + direction * direction
        grad = small[35:36, l * 256 : (l + 1) * 256]
        inner_g_ref[l : l + 1, :] = grad
        weight = inner_w_ref[l : l + 1, :]
        moment, direction = advance_one(grad, weight, inner_m_ref[l : l + 1, :])
        inner_m_out[l : l + 1, :] = moment
        inner_sums[0] = inner_sums[0] + weight * weight
        inner_sums[1] = inner_sums[1] + direction * direction
        for i in range(5):
            at = 8 * l + i
            grad = small_ref[at // 4, at // 2 % 2, 32:34, :].astype(F32)[at % 2 : at % 2 + 1]
            norm_g_ref[i, l : l + 1, :] = grad
            norm_m_out[i, l : l + 1, :] = MOMENTUM * norm_m_ref[i, l : l + 1, :] + grad
    for m in range(MP):
        rows = slice(m * 32, (m + 1) * 32)
        grad = small_ref[m // 2, m % 2, 0:32, :].astype(F32)
        embedding_g_ref[rows, :] = grad
        embedding_m_out[rows, :] = MOMENTUM * embedding_m_ref[rows, :] + grad

    ff_sums = (jnp.zeros((1, 256), F32), jnp.zeros((1, 256), F32))
    att_sums = (jnp.zeros((1, D), F32), jnp.zeros((1, D), F32))
    for l in range(2):
        loads[4 * l].wait()
        loads[4 * l + 1].wait()

        def ff_block(i, sums):
            mat = i // 8
            rows = pl.ds(pl.multiple_of(i % 8 * 64, 64), 64)
            weight = ff_w[l, mat, rows, :]
            rank = ff_rank[pl.ds(l * 16 + i, 1), :]
            grad = masked(ff_sum_ref[l, mat, rows, :].astype(F32), weight, rank)
            moment, direction = advance_one(grad, weight, ff_m[l, mat, rows, :])
            ff_g[l, mat, rows, :] = grad
            ff_m[l, mat, rows, :] = moment
            return sums[0] + square_sum(weight), sums[1] + square_sum(direction)

        ff_sums = lax.fori_loop(0, 16, ff_block, ff_sums)
        for i, (source, target) in enumerate(((ff_g, ff_g_hbm), (ff_m, ff_m_out))):
            copy = pltpu.make_async_copy(source.at[l], target.at[l], store_sem.at[4 * l + i])
            copy.start()
            stores.append(copy)
        loads[4 * l + 2].wait()
        loads[4 * l + 3].wait()

        def att_block(i, sums):
            weight = att_w[l, i]
            rank = att_rank[pl.ds(l * 5 + i, 1), :]
            grad = masked(att_sum_ref[l, i].astype(F32), weight, rank)
            moment, direction = advance_one(grad, weight, att_m[l, i])
            att_g[l, i] = grad
            att_m[l, i] = moment
            return sums[0] + square_sum(weight), sums[1] + square_sum(direction)

        att_sums = lax.fori_loop(0, 5, att_block, att_sums)
        for i, (source, target) in enumerate(((att_g, att_g_hbm), (att_m, att_m_out))):
            copy = pltpu.make_async_copy(source.at[l], target.at[l], store_sem.at[4 * l + 2 + i])
            copy.start()
            stores.append(copy)
    for k in range(2):
        for i, sums in enumerate((att_sums, ff_sums, head_sums, inner_sums)):
            part_ref[4 * k + i : 4 * k + i + 1, :] = jnp.broadcast_to(
                jnp.sum(sums[k], axis=1, keepdims=True), (1, 128)
            )
    memory_in.wait()
    memory_back = pltpu.make_async_copy(memory_ref, new_memory_out, memory_sem.at[1])
    memory_back.start()
    for copy in stores:
        copy.wait()
    memory_back.wait()


def moments(*operands):
    att, ff = (2, 5, HD, D), (2, 2, D, 256)
    outs = [
        (ANY_SPEC, att, F32),
        (ANY_SPEC, att, F32),
        (ANY_SPEC, ff, F32),
        (ANY_SPEC, ff, F32),
        (ANY_SPEC, (2, 4, SEG, D), BF16),
    ] + [
        (VMEM_SPEC, shape, F32)
        for shape in (
            (VOCAB, D),
            (VOCAB, D),
            (2, 2, HD),
            (2, 2, HD),
            (2, 256),
            (2, 256),
            (5, 2, D),
            (5, 2, D),
            (8, 128),
        )
    ]
    return pl.pallas_call(
        moments_kernel,
        out_shape=[jax.ShapeDtypeStruct(s, t) for _, s, t in outs],
        in_specs=[ANY_SPEC] * 5 + [VMEM_SPEC] * 11,
        out_specs=[m for m, _, _ in outs],
        scratch_shapes=[pltpu.VMEM(att, F32)] * 3
        + [pltpu.VMEM(ff, F32)] * 3
        + [
            pltpu.VMEM((10, D), F32),
            pltpu.VMEM((32, 256), F32),
            pltpu.VMEM((2, 4, SEG, D), BF16),
            pltpu.SemaphoreType.DMA((8,)),
            pltpu.SemaphoreType.DMA((8,)),
            pltpu.SemaphoreType.DMA((2,)),
        ],
        compiler_params=pltpu.CompilerParams(vmem_limit_bytes=62 * 1024 * 1024),
        name="moments",
    )(*operands)


def exchange_kernel(part_ref, out_ref, send_sem, recv_sem):
    here = Place()
    partners = [
        here.device(y=(here.y + s) % 4, core=(here.core + k) % 2)
        for s in range(4)
        for k in range(2)
        if s or k
    ]
    barrier = pltpu.get_barrier_semaphore()
    for partner in partners:
        pl.semaphore_signal(barrier, inc=1, device_id=partner, device_id_type=MESH)
    pl.semaphore_wait(barrier, len(partners))
    index = here.y * 2 + here.core
    out_ref[index] = part_ref[...]
    copies = [
        send(part_ref, out_ref.at[index], (send_sem, recv_sem), i, partner)
        for i, partner in enumerate(partners)
    ]
    for copy in copies:
        copy.wait()


def exchange(part):
    return pl.pallas_call(
        exchange_kernel,
        out_shape=jax.ShapeDtypeStruct((MP, 8, 128), F32),
        in_specs=[VMEM_SPEC],
        out_specs=VMEM_SPEC,
        scratch_shapes=[pltpu.SemaphoreType.DMA((7,)), pltpu.SemaphoreType.DMA((7,))],
        compiler_params=pltpu.CompilerParams(
            collective_id=2, has_side_effects=True, vmem_limit_bytes=62 * 1024 * 1024
        ),
        name="exchange",
    )(part)


def weights_kernel(*refs):
    inputs, outputs, scratch = refs[:25], refs[25:37], refs[37:]
    parts_ref = inputs[24]
    groups = [inputs[4 * i : 4 * i + 4] for i in range(6)]
    results = [outputs[2 * i : 2 * i + 2] for i in range(6)]
    buffers = [scratch[0:4], scratch[4:8]]
    load_sem, store_sem = scratch[8:10]
    loads = [
        [
            [
                pltpu.make_async_copy(
                    groups[g][i].at[l], buffers[g][i].at[l], load_sem.at[8 * g + 4 * l + i]
                )
                for i in range(4)
            ]
            for l in range(2)
        ]
        for g in range(2)
    ]
    for l in range(2):
        for g in (1, 0):
            for copy in loads[g][l]:
                copy.start()
    total = parts_ref[0]
    for m in range(1, MP):
        total = total + parts_ref[m]

    def rate(weight_square, direction_square):
        return RATE * (jnp.sqrt(weight_square) / jnp.sqrt(direction_square))

    def step(weight, grad, moment, average, ratio):
        weight_next = weight - ratio * (grad + MOMENTUM * moment)
        return weight_next, AVERAGE * average + (1.0 - AVERAGE) * weight_next

    ratios = [rate(total[i : i + 1, 0:1], total[4 + i : 5 + i, 0:1]) for i in range(4)]
    for l in range(2):
        for k in range(2):
            row = (l, slice(k, k + 1))
            new, mean = step(*[ref[row] for ref in groups[2]], ratios[2])
            results[2][0][row] = new
            results[2][1][row] = mean
    new, mean = step(*[ref[...] for ref in groups[3]], ratios[3])
    results[3][0][...] = new
    results[3][1][...] = mean
    squares = [jnp.zeros((1, D), F32), jnp.zeros((1, D), F32)]
    for b in range(4):
        rows = slice(b * 64, (b + 1) * 64)
        squares[0] = squares[0] + square_sum(groups[4][0][rows, :])
        squares[1] = squares[1] + square_sum(
            groups[4][1][rows, :] + MOMENTUM * groups[4][2][rows, :]
        )
    ratio = rate(*[jnp.sum(value, axis=1, keepdims=True) for value in squares])
    for b in range(4):
        rows = slice(b * 64, (b + 1) * 64)
        new, mean = step(*[ref[rows, :] for ref in groups[4]], ratio)
        results[4][0][rows, :] = new
        results[4][1][rows, :] = mean
    squares = [jnp.zeros((2, D), F32), jnp.zeros((2, D), F32)]
    for i in range(5):
        direction = groups[5][1][i] + MOMENTUM * groups[5][2][i]
        squares[0] = squares[0] + groups[5][0][i] * groups[5][0][i]
        squares[1] = squares[1] + direction * direction
    ratio = rate(
        *[jnp.sum(square_sum_rows(value), axis=1, keepdims=True) for value in squares]
    )
    for i in range(5):
        new, mean = step(*[ref[i] for ref in groups[5]], ratio)
        results[5][0][i] = new
        results[5][1][i] = mean

    stores = []
    for l in range(2):
        for g in (1, 0):
            for copy in loads[g][l]:
                copy.wait()
            weight, grad, moment, average = buffers[g]
            if g == 0:

                def block(i, carry):
                    new, mean = step(
                        weight[l, i], grad[l, i], moment[l, i], average[l, i], ratios[0]
                    )
                    weight[l, i] = new
                    average[l, i] = mean
                    return carry

                lax.fori_loop(0, 5, block, 0)
            else:

                def block(i, carry):
                    mat = i // 8
                    rows = pl.ds(pl.multiple_of(i % 8 * 64, 64), 64)
                    new, mean = step(
                        weight[l, mat, rows, :],
                        grad[l, mat, rows, :],
                        moment[l, mat, rows, :],
                        average[l, mat, rows, :],
                        ratios[1],
                    )
                    weight[l, mat, rows, :] = new
                    average[l, mat, rows, :] = mean
                    return carry

                lax.fori_loop(0, 16, block, 0)
            for k, source in enumerate((weight, average)):
                copy = pltpu.make_async_copy(
                    source.at[l], results[g][k].at[l], store_sem.at[4 * g + 2 * l + k]
                )
                copy.start()
                stores.append(copy)
    for copy in stores:
        copy.wait()


def square_sum_rows(value):
    return jnp.sum(value, axis=0, keepdims=True)


def new_weights(*operands):
    att, ff = (2, 5, HD, D), (2, 2, D, 256)
    shapes = [att, ff, (2, 2, HD), (2, 256), (VOCAB, D), (5, 2, D)]
    return pl.pallas_call(
        weights_kernel,
        out_shape=[jax.ShapeDtypeStruct(s, F32) for s in shapes for _ in range(2)],
        in_specs=[ANY_SPEC] * 8 + [VMEM_SPEC] * 17,
        out_specs=[ANY_SPEC] * 4 + [VMEM_SPEC] * 8,
        scratch_shapes=[pltpu.VMEM(att, F32)] * 4
        + [pltpu.VMEM(ff, F32)] * 4
        + [pltpu.SemaphoreType.DMA((16,)), pltpu.SemaphoreType.DMA((8,))],
        compiler_params=pltpu.CompilerParams(vmem_limit_bytes=62 * 1024 * 1024),
        name="new_weights",
    )(*operands)


def body(
    inputs,
    targets,
    valid_mask,
    memory,
    attention_rank,
    feedforward_rank,
    attention_weight,
    attention_moment,
    attention_average,
    feedforward_weight,
    feedforward_moment,
    feedforward_average,
    embedding_weight,
    embedding_moment,
    embedding_average,
    head_bias_weight,
    head_bias_moment,
    head_bias_average,
    inner_bias_weight,
    inner_bias_moment,
    inner_bias_average,
    norm_weight,
    norm_moment,
    norm_average,
):
    def turned(value):
        return value.transpose(0, 1, 3, 2)

    def swapped(value):
        return value.transpose(1, 0, 2)

    att_rank = attention_rank.reshape(10, 8).astype(F32)
    ff_rank = feedforward_rank.reshape(32, 4).astype(F32)
    table = tables()
    (
        att_got,
        ff_got,
        new_memory,
        probs,
        bias_got,
        count_got,
        lows,
        query_u,
        query_w,
        mixed,
        normed_one,
        inverse_one,
        normed_two,
        inverse_two,
        grad_hidden,
        grad_embedding,
        ce_local,
    ) = forward_all(
        turned(attention_weight),
        feedforward_weight,
        att_rank,
        ff_rank,
        head_bias_weight,
        inner_bias_weight,
        embedding_weight,
        inputs,
        targets,
        valid_mask,
        memory,
        swapped(norm_weight),
        table,
    )
    valid_count = count_got[0, 0]
    grad_attention, grad_feedforward, grad_small, ce_got = backward_all(
        att_got,
        ff_got,
        probs,
        memory,
        table,
        grad_hidden,
        grad_embedding,
        normed_two,
        bias_got,
        swapped(norm_weight),
        inputs,
        ce_local,
        lows,
        query_u,
        query_w,
        mixed,
        normed_one,
        inverse_one,
        inverse_two,
    )
    ce_total = ce_got[0, 0]
    (
        att_grad,
        att_moment,
        ff_grad,
        ff_moment,
        new_memory,
        embedding_grad,
        embedding_moment_next,
        head_grad,
        head_moment,
        inner_grad,
        inner_moment,
        norm_grad,
        norm_moment_next,
        part,
    ) = moments(
        turned(attention_weight),
        turned(attention_moment),
        feedforward_weight,
        feedforward_moment,
        new_memory,
        grad_attention,
        grad_feedforward,
        grad_small,
        att_rank,
        ff_rank,
        embedding_moment,
        head_bias_weight,
        head_bias_moment,
        inner_bias_weight,
        inner_bias_moment,
        swapped(norm_moment),
    )
    parts = exchange(part)
    (
        att_next,
        att_average,
        ff_next,
        ff_average,
        head_next,
        head_average,
        inner_next,
        inner_average,
        embedding_next,
        embedding_average_next,
        norm_next,
        norm_average_next,
    ) = new_weights(
        turned(attention_weight),
        att_grad,
        att_moment,
        turned(attention_average),
        feedforward_weight,
        ff_grad,
        ff_moment,
        feedforward_average,
        head_bias_weight,
        head_grad,
        head_moment,
        head_bias_average,
        inner_bias_weight,
        inner_grad,
        inner_moment,
        inner_bias_average,
        embedding_weight,
        embedding_grad,
        embedding_moment_next,
        embedding_average,
        swapped(norm_weight),
        norm_grad,
        norm_moment_next,
        swapped(norm_average),
        parts,
    )
    return (
        ce_total,
        valid_count,
        new_memory,
        turned(att_grad),
        turned(att_next),
        turned(att_moment),
        turned(att_average),
        ff_grad,
        ff_next,
        ff_moment,
        ff_average,
        embedding_next,
        embedding_moment_next,
        embedding_average_next,
        head_next,
        head_moment,
        head_average,
        inner_next,
        inner_moment,
        inner_average,
        swapped(norm_grad),
        swapped(norm_next),
        swapped(norm_moment_next),
        swapped(norm_average_next),
    )


def solution(mesh):
    rows = P("dp", None)
    matrix = P(None, None, None, "mp")
    split_two = P(None, None, "mp")
    split_one = P(None, "mp")
    whole = P()
    return jax.shard_map(
        body,
        mesh=mesh,
        in_specs=(
            (rows,) * 3
            + (P(None, "dp", None, None),)
            + (matrix,) * 8
            + (whole,) * 3
            + (split_two,) * 3
            + (split_one,) * 3
            + (whole,) * 3
        ),
        out_specs=(
            (whole,) * 2
            + (P(None, "dp", None, None),)
            + (matrix,) * 8
            + (whole,) * 3
            + (split_two,) * 3
            + (split_one,) * 3
            + (whole,) * 4
        ),
        check_vma=False,
    )
```

profile of v0, /device:TPU:1, one launch (start us, length us, event | category | flops | bytes accessed | tf_op | source)
XLA Modules:
  0.0 206.7 jit_solution(16622209716621788646)
XLA Ops:
  0.7 0.7 convert_reduce_fusion
  1.4 0.6 reshape.52.att_rank_ref
  2.0 0.7 convert_element_type.12
  2.7 0.7 copy.62
  3.4 76.6 %forward_all.1 = (bf16[2,5,2,4,64,512]{5,4,3,2,1,0:T(8,128)(2,1)}, bf16[2,2,2,4,512,256]{5,4,3,2,1,0:T(8,128)(2,1)}, bf16[2,4,512,512]{3,2,1,0:T(8,128)(2,1)}, f...) custom-call(f32[2,5,64,512]{3,2,1,0:T(8,128)} %bitcast.17, ...), custom_call_target="tpu_custom_call" | custom-call | tf_op jit(solution)/shard_map/forward_all/pallas_call | solution.py:593
  80.0 1.2 slice.7
  81.2 95.5 %backward_all.1 = (bf16[2,5,64,512]{3,2,1,0:T(8,128)(2,1)}, bf16[2,2,512,256]{3,2,1,0:T(8,128)(2,1)}, bf16[4,2,64,512]{3,2,1,0:T(8,128)(2,1)}, f32[8,128]{1,0:T(8,128)}) custom-call(bf16[2,5,2,4,64,512]{5,4,3,2,1,0:T(8,128)(2,1)} %get-tuple-element.71.att_hbm, bf16[2,2,2,4,512,256]{5,4,3,2,1,0:T(8,128)(2,1)} %get-tuple-element.72.ff_hbm, ...), custom_call_target="tpu_custom_call" | custom-call | tf_op jit(solution)/shard_map/backward_all/pallas_call | solution.py:1215
  176.7 1.2 slice.6
  177.9 11.9 %moments.1 = (f32[2,5,64,512]{3,2,1,0:T(8,128)}, f32[2,5,64,512]{3,2,1,0:T(8,128)}, f32[2,2,512,256]{3,2,1,0:T(8,128)}, f32[2,2,512,256]{3,2,1,0:T(8,128)}, bf16...) custom-call(f32[2,5,64,512]{3,2,1,0:T(8,128)} %bitcast.18, ...), custom_call_target="tpu_custom_call" | custom-call | tf_op jit(solution)/shard_map/moments/pallas_call | solution.py:1404
  189.8 6.5 %exchange.1.refs_24_ = f32[8,8,128]{2,1,0:T(8,128)} custom-call(f32[8,128]{1,0:T(8,128)} %get-tuple-element.105.part_ref), custom_call_target="tpu_custom_call" | custom-call | tf_op jit(solution)/shard_map/exchange/pallas_call | solution.py:1447
  196.2 10.3 %new_weights.1 = (f32[2,5,64,512]{3,2,1,0:T(8,128)}, f32[2,5,64,512]{3,2,1,0:T(8,128)}, f32[2,2,512,256]{3,2,1,0:T(8,128)}, f32[2,2,512,256]{3,2,1,0:T(8,128)}, ...) custom-call(f32[2,5,64,512]{3,2,1,0:T(8,128)} %bitcast.19, ...), custom_call_target="tpu_custom_call" | custom-call | tf_op jit(solution)/shard_map/new_weights/pallas_call | solution.py:1581
where the time goes:
time: 211 us; the launch traced here: 207 us
  Pallas kernels  201 us (95%)
  local copies, waits for them, and re-layouts  3.69 us (2%)
    pallas_call x1, Pallas kernels, backward_all(): pl.pallas_call(backward_step, out_shape=[jax.ShapeDtypeStruct(s, t) for s...  95.5 us
    pallas_call x1, Pallas kernels, forward_all(): pl.pallas_call(forward_step, out_shape=[jax.ShapeDtypeStruct(s, t) for _,...  76.6 us
    pallas_call x1, Pallas kernels, moments(): pl.pallas_call(moments_kernel, out_shape=[jax.ShapeDtypeStruct(s, t) for...  11.9 us
    pallas_call x1, Pallas kernels, new_weights(): pl.pallas_call(weights_kernel, out_shape=[jax.ShapeDtypeStruct(s, F32) fo...  10.3 us
    pallas_call x1, Pallas kernels, exchange(): pl.pallas_call(exchange_kernel, out_shape=jax.ShapeDtypeStruct((MP, 8, 12...  6.46 us

commit v1 on v0

--- a/solution.py
+++ b/solution.py
@@ -132,14 +132,15 @@
     def sibling(self):
         return self.device(core=1 - self.core)
 
-    def greet(self):
-        partners = [self.along(axis, s) for axis in "xzy" for s in (1, 2, 3)] + [self.sibling()]
+    def greet(self, more=()):
+        partners = [self.along(axis, s) for axis in "xzy" for s in (1, 2, 3)]
+        partners += [self.sibling(), *more]
         barrier = pltpu.get_barrier_semaphore()
         for partner in partners:
             pl.semaphore_signal(barrier, inc=1, device_id=partner, device_id_type=MESH)
 
-    def greeted(self):
-        pl.semaphore_wait(pltpu.get_barrier_semaphore(), 10)
+    def greeted(self, count=10):
+        pl.semaphore_wait(pltpu.get_barrier_semaphore(), count)
 
 
 def send(source, target, sems, index, device):
@@ -160,6 +161,20 @@
     lane = lax.broadcasted_iota(jnp.int32, (blocks, width), 1) // (width // blocks)
     row = lax.broadcasted_iota(jnp.int32, (blocks, width), 0)
     return dot_nn(rank, jnp.where(lane == row, 1.0, 0.0))
+
+
+def advance_one(grad, weight, moment):
+    moment_next = MOMENTUM * moment + grad
+    return moment_next, grad + MOMENTUM * moment_next
+
+
+def masked(grad, weight, rank):
+    coefficient = jnp.where(rank < 1.5, 1.0, jnp.where(rank < 2.5, WIDEN, 0.0))
+    return jnp.where(rank < 2.5, grad, 0.0) + (2.0 * PENALTY) * weight * coefficient
+
+
+def square_sum(value):
+    return jnp.sum(value * value, axis=0, keepdims=True)
 
 
 class Weights:
@@ -773,6 +788,16 @@
     grad_hbm,
     grad_embedding_hbm,
     normed_two_hbm,
+    att_weight_hbm,
+    att_moment_hbm,
+    ff_weight_hbm,
+    ff_moment_hbm,
+    att_rank_ref,
+    ff_rank_ref,
+    head_weight_ref,
+    head_moment_ref,
+    inner_weight_ref,
+    inner_moment_ref,
     bias_ref,
     norm_ref,
     inputs_ref,
@@ -788,6 +813,7 @@
     ff_out,
     small_out,
     ce_out,
+    parts_out,
     att_w,
     ff_w,
     memory_w,
@@ -823,6 +849,9 @@
     ce_y,
     ce_x,
     small_own,
+    rank_ref,
+    block_rank_ref,
+    part_ref,
     *scratch,
 ):
     here = Place()
@@ -832,8 +861,8 @@
     for group in SUM_GROUPS:
         for buffers in (ones, twos, threes):
             buffers.append([scratch.pop(0) for _ in group[3]])
-    sems = [(scratch.pop(0), scratch.pop(0)) for _ in range(6)]
-    load_sem, prob_sem = scratch
+    sems = [(scratch.pop(0), scratch.pop(0)) for _ in range(7)]
+    load_sem, prob_sem, stage_sem = scratch
     extra = sems[5]
     sums = Sums(
         here,
@@ -860,8 +889,16 @@
     load_att.start()
     for copy in loads:
         copy.start()
-    here.greet()
-    here.greeted()
+    others = [
+        here.device(y=(here.y + s) % 4, core=(here.core + k) % 2)
+        for s in range(4)
+        for k in range(2)
+        if s or k
+    ]
+    here.greet(others[2::2])
+    rank_ref[...] = spread_rank(att_rank_ref[...], D)
+    block_rank_ref[...] = spread_rank(ff_rank_ref[...], 256)
+    here.greeted(13)
     own_rows = pl.ds(pl.multiple_of(here.core * OWN, OWN), OWN)
     their_rows = pl.ds(pl.multiple_of(OWN - here.core * OWN, OWN), OWN)
     ce_pair[here.core] = ce_ref[...]
@@ -1097,6 +1134,78 @@
     sums.three(2)
     finish(swaps_zero)
 
+    def stage(pairs, slot):
+        copies = []
+        for i, (source, target) in enumerate(pairs):
+            copies.append(pltpu.make_async_copy(source, target, stage_sem.at[10 * slot + i]))
+            copies[-1].start()
+        return copies
+
+    def stage_ff(layer, mat):
+        return stage(
+            [
+                (
+                    source.at[layer, mat, 256 * i : 256 * i + 256],
+                    prob_ref.at[mat, :, 512 * k + 256 * i : 512 * k + 256 * i + 256],
+                )
+                for k, source in enumerate((ff_weight_hbm, ff_moment_hbm))
+                for i in range(2)
+            ],
+            mat,
+        )
+
+    def stage_att(layer):
+        pairs = []
+        for k, source in enumerate((att_weight_hbm, att_moment_hbm)):
+            cols = slice(512 * k, 512 * k + 512)
+            for i in range(4):
+                pairs.append(
+                    (source.at[layer, i], prob_ref.at[layer, 64 * i : 64 * i + 64, cols])
+                )
+            rows = slice(64 * layer, 64 * layer + 64)
+            pairs.append((source.at[layer, 4], prob_grad_ref.at[rows, cols]))
+        return stage(pairs, layer)
+
+    squares = {ATT: [jnp.zeros((1, D), F32)] * 2, FFN: [jnp.zeros((1, 256), F32)] * 2}
+
+    def add_squares(kind, total, weight, moment, rank):
+        grad = masked(total.astype(F32), weight, rank)
+        _, direction = advance_one(grad, weight, moment)
+        first, second = squares[kind]
+        squares[kind] = [first + square_sum(weight), second + square_sum(direction)]
+
+    def square_ff(layer, copies):
+        for copy in copies:
+            copy.wait()
+        for mat in range(2):
+            for i in range(8):
+                rows = slice(i % 4 * 64, i % 4 * 64 + 64)
+                col = i // 4 * 256
+                rank_at = layer * 16 + mat * 8 + i
+                add_squares(
+                    FFN,
+                    ff_out[layer, mat, i * 64 : i * 64 + 64, :],
+                    prob_ref[mat, rows, col : col + 256],
+                    prob_ref[mat, rows, 512 + col : 768 + col],
+                    block_rank_ref[rank_at : rank_at + 1, :],
+                )
+
+    def square_att(layer, copies):
+        for copy in copies:
+            copy.wait()
+        for i in range(5):
+            rows = slice(64 * i, 64 * i + 64) if i < 4 else slice(64 * layer, 64 * layer + 64)
+            block = prob_ref.at[layer, rows] if i < 4 else prob_grad_ref.at[rows]
+            add_squares(
+                ATT,
+                att_out[layer, i],
+                block[:, 0:512],
+                block[:, 512:1024],
+                rank_ref[layer * 5 + i : layer * 5 + i + 1, :],
+            )
+
+    staged = stage_ff(1, 0) + stage_ff(1, 1)
+
     tokens = inputs_ref[pl.ds(here.y, 1), own_rows]
     onehot = jnp.where(
         tokens == lax.broadcasted_iota(jnp.int32, (VOCAB, OWN), 0), 1.0, 0.0
@@ -1133,6 +1242,9 @@
     sums.three(5)
     sums.two(4)
     sums.four(2)
+    sums.arrived(4, 3)
+    square_ff(1, staged)
+    staged = stage_ff(0, 0) + stage_ff(0, 1)
     sums.three(0)
     sums.three(4)
     sums.four(1)
@@ -1142,17 +1254,53 @@
     ce_out[...] = (ce_x[0] + ce_x[1]) + (ce_x[2] + ce_x[3])
     sums.four(4)
     sums.four(0)
+    sums.arrived(4, 1)
+    square_ff(0, staged)
+    staged_one, staged_zero = stage_att(1), stage_att(0)
     sums.arrived(4, 4)
     small_out[here.y, here.core] = small_own[0, 0]
     piece = small_out.at[here.y, here.core]
     small_copies = [send(piece, piece, extra, 13 + r, here.along("y", r)) for r in (1, 2, 3)]
+    small = small_own[0, 0].astype(F32)
+    head_sums = [jnp.zeros((1, HD), F32)] * 2
+    inner_sums = [jnp.zeros((1, 256), F32)] * 2
+    for l in range(2):
+        for k in range(2):
+            at = (l * 2 + k) * HD
+            weight = head_weight_ref[l, k : k + 1, :]
+            _, direction = advance_one(
+                small[34:35, at : at + HD], weight, head_moment_ref[l, k : k + 1, :]
+            )
+            head_sums = [head_sums[0] + weight * weight, head_sums[1] + direction * direction]
+        weight = inner_weight_ref[l : l + 1, :]
+        _, direction = advance_one(
+            small[35:36, l * 256 : (l + 1) * 256], weight, inner_moment_ref[l : l + 1, :]
+        )
+        inner_sums = [inner_sums[0] + weight * weight, inner_sums[1] + direction * direction]
+    sums.arrived(4, 2)
+    sums.arrived(4, 6)
+    square_att(1, staged_one)
     for copy in small_copies:
         copy.wait_recv()
     piece = small_out.at[:, here.core]
     last = send(piece, piece, extra, 17, here.sibling())
-    for g in (3, 6, 2, 1, 5, 0):
-        sums.arrived(4, g)
+    sums.arrived(4, 5)
+    sums.arrived(4, 0)
+    square_att(0, staged_zero)
+    for k in range(2):
+        for i, value in enumerate((squares[ATT], squares[FFN], head_sums, inner_sums)):
+            part_ref[4 * k + i : 4 * k + i + 1, :] = jnp.broadcast_to(
+                jnp.sum(value[k], axis=1, keepdims=True), (1, 128)
+            )
+    index = here.y * 2 + here.core
+    parts_out[index] = part_ref[...]
+    norm_copies = [
+        send(part_ref, parts_out.at[index], sems[6], i, partner)
+        for i, partner in enumerate(others)
+    ]
     last.wait()
+    for copy in norm_copies:
+        copy.wait()
     for copy in ce_copies + swaps_zero + small_copies:
         copy.wait_send()
     sums.end()
@@ -1165,6 +1313,7 @@
         ((2, 2, D, 256), BF16),
         ((4, 2, 64, D), BF16),
         ((8, 128), F32),
+        ((MP, 8, 128), F32),
     ]
     scratch = [
         pltpu.VMEM((5, 2, 4, HD, D), BF16),
@@ -1202,6 +1351,9 @@
         pltpu.VMEM((4, 8, 128), F32),
         pltpu.VMEM((4, 8, 128), F32),
         pltpu.VMEM((1, 1, 64, D), BF16),
+        pltpu.VMEM((10, D), F32),
+        pltpu.VMEM((32, 256), F32),
+        pltpu.VMEM((8, 128), F32),
     ]
     scratch += [pltpu.VMEM((hi - lo, 4) + SHAPES[k], BF16) for k, _, (lo, hi), _, _ in SUM_GROUPS]
     for kind, _, _, parts, rows in SUM_GROUPS:
@@ -1209,14 +1361,14 @@
         scratch += [pltpu.VMEM((3, hi - lo, 4, rows, width), BF16) for _, lo, hi in parts]
         scratch += [pltpu.VMEM((3, hi - lo, rows, width), BF16) for _, lo, hi in parts]
         scratch += [pltpu.VMEM((4, hi - lo, rows, width), BF16) for _, lo, hi in parts]
-    for n in (7, 42, 42, 42, 42, 18):
+    for n in (7, 42, 42, 42, 42, 18, 7):
         scratch += [pltpu.SemaphoreType.DMA((n,)), pltpu.SemaphoreType.DMA((n,))]
-    scratch += [pltpu.SemaphoreType.DMA((8,)), pltpu.SemaphoreType.DMA((2,))]
+    scratch += [pltpu.SemaphoreType.DMA((n,)) for n in (8, 2, 20)]
     return pl.pallas_call(
         backward_step,
         out_shape=[jax.ShapeDtypeStruct(s, t) for s, t in outs],
-        in_specs=[hbm] * 8 + [vmem] * 11,
-        out_specs=[vmem] * 4,
+        in_specs=[hbm] * 12 + [vmem] * 17,
+        out_specs=[vmem] * 5,
         scratch_shapes=scratch,
         compiler_params=pltpu.CompilerParams(
             collective_id=1, has_side_effects=True, vmem_limit_bytes=63 * 1024 * 1024
@@ -1225,152 +1377,148 @@
     )(*operands)
 
 
-def advance_one(grad, weight, moment):
-    moment_next = MOMENTUM * moment + grad
-    return moment_next, grad + MOMENTUM * moment_next
-
-
-def masked(grad, weight, rank):
-    coefficient = jnp.where(rank < 1.5, 1.0, jnp.where(rank < 2.5, WIDEN, 0.0))
-    return jnp.where(rank < 2.5, grad, 0.0) + (2.0 * PENALTY) * weight * coefficient
-
-
-def square_sum(value):
-    return jnp.sum(value * value, axis=0, keepdims=True)
-
-
-def moments_kernel(
-    att_w_hbm,
-    att_m_hbm,
-    ff_w_hbm,
-    ff_m_hbm,
-    new_memory_hbm,
-    att_sum_ref,
-    ff_sum_ref,
-    small_ref,
-    att_rank_ref,
-    ff_rank_ref,
-    embedding_m_ref,
-    head_w_ref,
-    head_m_ref,
-    inner_w_ref,
-    inner_m_ref,
-    norm_m_ref,
-    att_g_hbm,
-    att_m_out,
-    ff_g_hbm,
-    ff_m_out,
-    new_memory_out,
-    embedding_g_ref,
-    embedding_m_out,
-    head_g_ref,
-    head_m_out,
-    inner_g_ref,
-    inner_m_out,
-    norm_g_ref,
-    norm_m_out,
-    part_ref,
-    att_w,
-    att_m,
-    att_g,
-    ff_w,
-    ff_m,
-    ff_g,
-    att_rank,
-    ff_rank,
-    memory_ref,
-    load_sem,
-    store_sem,
-    memory_sem,
-):
+def update_kernel(*refs):
+    (
+        att_w_hbm,
+        att_m_hbm,
+        att_a_hbm,
+        ff_w_hbm,
+        ff_m_hbm,
+        ff_a_hbm,
+        new_memory_hbm,
+        att_sum_ref,
+        ff_sum_ref,
+        small_ref,
+        parts_ref,
+        att_rank_ref,
+        ff_rank_ref,
+        *rest,
+    ) = refs[:25]
+    embedding, head, inner, norm = (rest[3 * i : 3 * i + 3] for i in range(4))
+    outs = refs[25:47]
+    att_outs, ff_outs, new_memory_out = outs[0:4], outs[4:8], outs[8]
+    embedding_outs, head_outs, inner_outs, norm_outs = (
+        outs[9:12],
+        outs[12:15],
+        outs[15:18],
+        outs[18:22],
+    )
+    att, ff = refs[47:51], refs[51:55]
+    att_rank, ff_rank, memory_ref, load_sem, store_sem, memory_sem = refs[55:]
     loads, stores = [], []
     for l in range(2):
-        for i, (source, target) in enumerate(
-            ((ff_w_hbm, ff_w), (ff_m_hbm, ff_m), (att_w_hbm, att_w), (att_m_hbm, att_m))
+        for k, (sources, targets) in enumerate(
+            (((ff_w_hbm, ff_m_hbm, ff_a_hbm), ff), ((att_w_hbm, att_m_hbm, att_a_hbm), att))
         ):
-            copy = pltpu.make_async_copy(source.at[l], target.at[l], load_sem.at[4 * l + i])
-            copy.start()
-            loads.append(copy)
+            for i in range(3):
+                copy = pltpu.make_async_copy(
+                    sources[i].at[l], targets[i].at[l], load_sem.at[6 * l + 3 * k + i]
+                )
+                copy.start()
+                loads.append(copy)
     memory_in = pltpu.make_async_copy(new_memory_hbm, memory_ref, memory_sem.at[0])
     memory_in.start()
     att_rank[...] = spread_rank(att_rank_ref[...], D)
     ff_rank[...] = spread_rank(ff_rank_ref[...], 256)
+    total = parts_ref[0]
+    for m in range(1, MP):
+        total = total + parts_ref[m]
+
+    def rate(weight_square, direction_square):
+        return RATE * (jnp.sqrt(weight_square) / jnp.sqrt(direction_square))
+
+    def step(weight, direction, average, ratio):
+        weight_next = weight - ratio * direction
+        return weight_next, AVERAGE * average + (1.0 - AVERAGE) * weight_next
+
+    ratios = [rate(total[i : i + 1, 0:1], total[4 + i : 5 + i, 0:1]) for i in range(4)]
 
     small = small_ref[lax.axis_index("mp") // 2, lax.axis_index("mp") % 2].astype(F32)
-    head_sums = [jnp.zeros((1, HD), F32)] * 2
-    inner_sums = [jnp.zeros((1, 256), F32)] * 2
     for l in range(2):
         for k in range(2):
             at = (l * 2 + k) * HD
-            grad = small[34:35, at : at + HD]
-            head_g_ref[l, k : k + 1, :] = grad
-            weight = head_w_ref[l, k : k + 1, :]
-            moment, direction = advance_one(grad, weight, head_m_ref[l, k : k + 1, :])
-            head_m_out[l, k : k + 1, :] = moment
-            head_sums[0] = head_sums[0] + weight * weight
-            head_sums[1] = head_sums[1] + direction * direction
-        grad = small[35:36, l * 256 : (l + 1) * 256]
-        inner_g_ref[l : l + 1, :] = grad
-        weight = inner_w_ref[l : l + 1, :]
-        moment, direction = advance_one(grad, weight, inner_m_ref[l : l + 1, :])
-        inner_m_out[l : l + 1, :] = moment
-        inner_sums[0] = inner_sums[0] + weight * weight
-        inner_sums[1] = inner_sums[1] + direction * direction
-        for i in range(5):
+            row = (l, slice(k, k + 1))
+            moment, direction = advance_one(small[34:35, at : at + HD], head[0][row], head[1][row])
+            head_outs[1][row] = moment
+            head_outs[0][row], head_outs[2][row] = step(
+                head[0][row], direction, head[2][row], ratios[2]
+            )
+        row = slice(l, l + 1)
+        moment, direction = advance_one(
+            small[35:36, l * 256 : (l + 1) * 256], inner[0][row], inner[1][row]
+        )
+        inner_outs[1][row] = moment
+        inner_outs[0][row], inner_outs[2][row] = step(
+            inner[0][row], direction, inner[2][row], ratios[3]
+        )
+    squares = [jnp.zeros((1, D), F32), jnp.zeros((1, D), F32)]
+    for i in range(5):
+        for l in range(2):
             at = 8 * l + i
+            row = (i, slice(l, l + 1))
             grad = small_ref[at // 4, at // 2 % 2, 32:34, :].astype(F32)[at % 2 : at % 2 + 1]
-            norm_g_ref[i, l : l + 1, :] = grad
-            norm_m_out[i, l : l + 1, :] = MOMENTUM * norm_m_ref[i, l : l + 1, :] + grad
+            moment, direction = advance_one(grad, norm[0][row], norm[1][row])
+            norm_outs[0][row] = grad
+            norm_outs[2][row] = moment
+            squares[0] = squares[0] + norm[0][row] * norm[0][row]
+            squares[1] = squares[1] + direction * direction
+    ratio = rate(*[jnp.sum(value, axis=1, keepdims=True) for value in squares])
+    for i in range(5):
+        direction = norm_outs[0][i] + MOMENTUM * norm_outs[2][i]
+        norm_outs[1][i], norm_outs[3][i] = step(norm[0][i], direction, norm[2][i], ratio)
+    squares = [jnp.zeros((1, D), F32), jnp.zeros((1, D), F32)]
     for m in range(MP):
         rows = slice(m * 32, (m + 1) * 32)
         grad = small_ref[m // 2, m % 2, 0:32, :].astype(F32)
-        embedding_g_ref[rows, :] = grad
-        embedding_m_out[rows, :] = MOMENTUM * embedding_m_ref[rows, :] + grad
-
-    ff_sums = (jnp.zeros((1, 256), F32), jnp.zeros((1, 256), F32))
-    att_sums = (jnp.zeros((1, D), F32), jnp.zeros((1, D), F32))
+        moment, direction = advance_one(grad, embedding[0][rows], embedding[1][rows])
+        embedding_outs[1][rows] = moment
+        squares[0] = squares[0] + square_sum(embedding[0][rows])
+        squares[1] = squares[1] + square_sum(direction)
+    ratio = rate(*[jnp.sum(value, axis=1, keepdims=True) for value in squares])
+    for m in range(MP):
+        rows = slice(m * 32, (m + 1) * 32)
+        grad = small_ref[m // 2, m % 2, 0:32, :].astype(F32)
+        direction = grad + MOMENTUM * embedding_outs[1][rows]
+        embedding_outs[0][rows], embedding_outs[2][rows] = step(
+            embedding[0][rows], direction, embedding[2][rows], ratio
+        )
+
+    def advance(refs, at, total, rank, ratio):
+        weight, moment, average, grad_ref = refs
+        grad = masked(total.astype(F32), weight[at], rank)
+        moment_next, direction = advance_one(grad, weight[at], moment[at])
+        grad_ref[at] = grad
+        moment[at] = moment_next
+        weight[at], average[at] = step(weight[at], direction, average[at], ratio)
+
     for l in range(2):
-        loads[4 * l].wait()
-        loads[4 * l + 1].wait()
-
-        def ff_block(i, sums):
-            mat = i // 8
-            rows = pl.ds(pl.multiple_of(i % 8 * 64, 64), 64)
-            weight = ff_w[l, mat, rows, :]
-            rank = ff_rank[pl.ds(l * 16 + i, 1), :]
-            grad = masked(ff_sum_ref[l, mat, rows, :].astype(F32), weight, rank)
-            moment, direction = advance_one(grad, weight, ff_m[l, mat, rows, :])
-            ff_g[l, mat, rows, :] = grad
-            ff_m[l, mat, rows, :] = moment
-            return sums[0] + square_sum(weight), sums[1] + square_sum(direction)
-
-        ff_sums = lax.fori_loop(0, 16, ff_block, ff_sums)
-        for i, (source, target) in enumerate(((ff_g, ff_g_hbm), (ff_m, ff_m_out))):
-            copy = pltpu.make_async_copy(source.at[l], target.at[l], store_sem.at[4 * l + i])
-            copy.start()
-            stores.append(copy)
-        loads[4 * l + 2].wait()
-        loads[4 * l + 3].wait()
-
-        def att_block(i, sums):
-            weight = att_w[l, i]
-            rank = att_rank[pl.ds(l * 5 + i, 1), :]
-            grad = masked(att_sum_ref[l, i].astype(F32), weight, rank)
-            moment, direction = advance_one(grad, weight, att_m[l, i])
-            att_g[l, i] = grad
-            att_m[l, i] = moment
-            return sums[0] + square_sum(weight), sums[1] + square_sum(direction)
-
-        att_sums = lax.fori_loop(0, 5, att_block, att_sums)
-        for i, (source, target) in enumerate(((att_g, att_g_hbm), (att_m, att_m_out))):
-            copy = pltpu.make_async_copy(source.at[l], target.at[l], store_sem.at[4 * l + 2 + i])
-            copy.start()
-            stores.append(copy)
-    for k in range(2):
-        for i, sums in enumerate((att_sums, ff_sums, head_sums, inner_sums)):
-            part_ref[4 * k + i : 4 * k + i + 1, :] = jnp.broadcast_to(
-                jnp.sum(sums[k], axis=1, keepdims=True), (1, 128)
-            )
+        for k in range(2):
+            for i in range(3):
+                loads[6 * l + 3 * k + i].wait()
+            if k == 0:
+
+                def block(i, carry):
+                    at = (l, i // 8, pl.ds(pl.multiple_of(i % 8 * 64, 64), 64))
+                    rank = ff_rank[pl.ds(l * 16 + i, 1), :]
+                    advance(ff, at, ff_sum_ref[at], rank, ratios[1])
+                    return carry
+
+                lax.fori_loop(0, 16, block, 0)
+            else:
+
+                def block(i, carry):
+                    rank = att_rank[pl.ds(l * 5 + i, 1), :]
+                    advance(att, (l, i), att_sum_ref[l, i], rank, ratios[0])
+                    return carry
+
+                lax.fori_loop(0, 5, block, 0)
+            sources, targets = ((ff, ff_outs), (att, att_outs))[k]
+            for i, source in enumerate((3, 0, 1, 2)):
+                copy = pltpu.make_async_copy(
+                    sources[source].at[l], targets[i].at[l], store_sem.at[8 * l + 4 * k + i]
+                )
+                copy.start()
+                stores.append(copy)
     memory_in.wait()
     memory_back = pltpu.make_async_copy(memory_ref, new_memory_out, memory_sem.at[1])
     memory_back.start()
@@ -1379,215 +1527,29 @@
     memory_back.wait()
 
 
-def moments(*operands):
+def update(*operands):
     att, ff = (2, 5, HD, D), (2, 2, D, 256)
-    outs = [
-        (ANY_SPEC, att, F32),
-        (ANY_SPEC, att, F32),
-        (ANY_SPEC, ff, F32),
-        (ANY_SPEC, ff, F32),
-        (ANY_SPEC, (2, 4, SEG, D), BF16),
-    ] + [
-        (VMEM_SPEC, shape, F32)
-        for shape in (
-            (VOCAB, D),
-            (VOCAB, D),
-            (2, 2, HD),
-            (2, 2, HD),
-            (2, 256),
-            (2, 256),
-            (5, 2, D),
-            (5, 2, D),
-            (8, 128),
-        )
-    ]
+    shapes = [att] * 4 + [ff] * 4
+    rest = [(VOCAB, D)] * 3 + [(2, 2, HD)] * 3 + [(2, 256)] * 3 + [(5, 2, D)] * 4
     return pl.pallas_call(
-        moments_kernel,
-        out_shape=[jax.ShapeDtypeStruct(s, t) for _, s, t in outs],
-        in_specs=[ANY_SPEC] * 5 + [VMEM_SPEC] * 11,
-        out_specs=[m for m, _, _ in outs],
-        scratch_shapes=[pltpu.VMEM(att, F32)] * 3
-        + [pltpu.VMEM(ff, F32)] * 3
+        update_kernel,
+        out_shape=[jax.ShapeDtypeStruct(s, F32) for s in shapes]
+        + [jax.ShapeDtypeStruct((2, 4, SEG, D), BF16)]
+        + [jax.ShapeDtypeStruct(s, F32) for s in rest],
+        in_specs=[ANY_SPEC] * 7 + [VMEM_SPEC] * 18,
+        out_specs=[ANY_SPEC] * 9 + [VMEM_SPEC] * 13,
+        scratch_shapes=[pltpu.VMEM(att, F32)] * 4
+        + [pltpu.VMEM(ff, F32)] * 4
         + [
             pltpu.VMEM((10, D), F32),
             pltpu.VMEM((32, 256), F32),
             pltpu.VMEM((2, 4, SEG, D), BF16),
-            pltpu.SemaphoreType.DMA((8,)),
-            pltpu.SemaphoreType.DMA((8,)),
+            pltpu.SemaphoreType.DMA((12,)),
+            pltpu.SemaphoreType.DMA((16,)),
             pltpu.SemaphoreType.DMA((2,)),
         ],
         compiler_params=pltpu.CompilerParams(vmem_limit_bytes=62 * 1024 * 1024),
-        name="moments",
-    )(*operands)
-
-
-def exchange_kernel(part_ref, out_ref, send_sem, recv_sem):
-    here = Place()
-    partners = [
-        here.device(y=(here.y + s) % 4, core=(here.core + k) % 2)
-        for s in range(4)
-        for k in range(2)
-        if s or k
-    ]
-    barrier = pltpu.get_barrier_semaphore()
-    for partner in partners:
-        pl.semaphore_signal(barrier, inc=1, device_id=partner, device_id_type=MESH)
-    pl.semaphore_wait(barrier, len(partners))
-    index = here.y * 2 + here.core
-    out_ref[index] = part_ref[...]
-    copies = [
-        send(part_ref, out_ref.at[index], (send_sem, recv_sem), i, partner)
-        for i, partner in enumerate(partners)
-    ]
-    for copy in copies:
-        copy.wait()
-
-
-def exchange(part):
-    return pl.pallas_call(
-        exchange_kernel,
-        out_shape=jax.ShapeDtypeStruct((MP, 8, 128), F32),
-        in_specs=[VMEM_SPEC],
-        out_specs=VMEM_SPEC,
-        scratch_shapes=[pltpu.SemaphoreType.DMA((7,)), pltpu.SemaphoreType.DMA((7,))],
-        compiler_params=pltpu.CompilerParams(
-            collective_id=2, has_side_effects=True, vmem_limit_bytes=62 * 1024 * 1024
-        ),
-        name="exchange",
-    )(part)
-
-
-def weights_kernel(*refs):
-    inputs, outputs, scratch = refs[:25], refs[25:37], refs[37:]
-    parts_ref = inputs[24]
-    groups = [inputs[4 * i : 4 * i + 4] for i in range(6)]
-    results = [outputs[2 * i : 2 * i + 2] for i in range(6)]
-    buffers = [scratch[0:4], scratch[4:8]]
-    load_sem, store_sem = scratch[8:10]
-    loads = [
-        [
-            [
-                pltpu.make_async_copy(
-                    groups[g][i].at[l], buffers[g][i].at[l], load_sem.at[8 * g + 4 * l + i]
-                )
-                for i in range(4)
-            ]
-            for l in range(2)
-        ]
-        for g in range(2)
-    ]
-    for l in range(2):
-        for g in (1, 0):
-            for copy in loads[g][l]:
-                copy.start()
-    total = parts_ref[0]
-    for m in range(1, MP):
-        total = total + parts_ref[m]
-
-    def rate(weight_square, direction_square):
-        return RATE * (jnp.sqrt(weight_square) / jnp.sqrt(direction_square))
-
-    def step(weight, grad, moment, average, ratio):
-        weight_next = weight - ratio * (grad + MOMENTUM * moment)
-        return weight_next, AVERAGE * average + (1.0 - AVERAGE) * weight_next
-
-    ratios = [rate(total[i : i + 1, 0:1], total[4 + i : 5 + i, 0:1]) for i in range(4)]
-    for l in range(2):
-        for k in range(2):
-            row = (l, slice(k, k + 1))
-            new, mean = step(*[ref[row] for ref in groups[2]], ratios[2])
-            results[2][0][row] = new
-            results[2][1][row] = mean
-    new, mean = step(*[ref[...] for ref in groups[3]], ratios[3])
-    results[3][0][...] = new
-    results[3][1][...] = mean
-    squares = [jnp.zeros((1, D), F32), jnp.zeros((1, D), F32)]
-    for b in range(4):
-        rows = slice(b * 64, (b + 1) * 64)
-        squares[0] = squares[0] + square_sum(groups[4][0][rows, :])
-        squares[1] = squares[1] + square_sum(
-            groups[4][1][rows, :] + MOMENTUM * groups[4][2][rows, :]
-        )
-    ratio = rate(*[jnp.sum(value, axis=1, keepdims=True) for value in squares])
-    for b in range(4):
-        rows = slice(b * 64, (b + 1) * 64)
-        new, mean = step(*[ref[rows, :] for ref in groups[4]], ratio)
-        results[4][0][rows, :] = new
-        results[4][1][rows, :] = mean
-    squares = [jnp.zeros((2, D), F32), jnp.zeros((2, D), F32)]
-    for i in range(5):
-        direction = groups[5][1][i] + MOMENTUM * groups[5][2][i]
-        squares[0] = squares[0] + groups[5][0][i] * groups[5][0][i]
-        squares[1] = squares[1] + direction * direction
-    ratio = rate(
-        *[jnp.sum(square_sum_rows(value), axis=1, keepdims=True) for value in squares]
-    )
-    for i in range(5):
-        new, mean = step(*[ref[i] for ref in groups[5]], ratio)
-        results[5][0][i] = new
-        results[5][1][i] = mean
-
-    stores = []
-    for l in range(2):
-        for g in (1, 0):
-            for copy in loads[g][l]:
-                copy.wait()
-            weight, grad, moment, average = buffers[g]
-            if g == 0:
-
-                def block(i, carry):
-                    new, mean = step(
-                        weight[l, i], grad[l, i], moment[l, i], average[l, i], ratios[0]
-                    )
-                    weight[l, i] = new
-                    average[l, i] = mean
-                    return carry
-
-                lax.fori_loop(0, 5, block, 0)
-            else:
-
-                def block(i, carry):
-                    mat = i // 8
-                    rows = pl.ds(pl.multiple_of(i % 8 * 64, 64), 64)
-                    new, mean = step(
-                        weight[l, mat, rows, :],
-                        grad[l, mat, rows, :],
-                        moment[l, mat, rows, :],
-                        average[l, mat, rows, :],
-                        ratios[1],
-                    )
-                    weight[l, mat, rows, :] = new
-                    average[l, mat, rows, :] = mean
-                    return carry
-
-                lax.fori_loop(0, 16, block, 0)
-            for k, source in enumerate((weight, average)):
-                copy = pltpu.make_async_copy(
-                    source.at[l], results[g][k].at[l], store_sem.at[4 * g + 2 * l + k]
-                )
-                copy.start()
-                stores.append(copy)
-    for copy in stores:
-        copy.wait()
-
-
-def square_sum_rows(value):
-    return jnp.sum(value, axis=0, keepdims=True)
-
-
-def new_weights(*operands):
-    att, ff = (2, 5, HD, D), (2, 2, D, 256)
-    shapes = [att, ff, (2, 2, HD), (2, 256), (VOCAB, D), (5, 2, D)]
-    return pl.pallas_call(
-        weights_kernel,
-        out_shape=[jax.ShapeDtypeStruct(s, F32) for s in shapes for _ in range(2)],
-        in_specs=[ANY_SPEC] * 8 + [VMEM_SPEC] * 17,
-        out_specs=[ANY_SPEC] * 4 + [VMEM_SPEC] * 8,
-        scratch_shapes=[pltpu.VMEM(att, F32)] * 4
-        + [pltpu.VMEM(ff, F32)] * 4
-        + [pltpu.SemaphoreType.DMA((16,)), pltpu.SemaphoreType.DMA((8,))],
-        compiler_params=pltpu.CompilerParams(vmem_limit_bytes=62 * 1024 * 1024),
-        name="new_weights",
+        name="update",
     )(*operands)
 
 
@@ -1660,7 +1622,7 @@
         table,
     )
     valid_count = count_got[0, 0]
-    grad_attention, grad_feedforward, grad_small, ce_got = backward_all(
+    grad_attention, grad_feedforward, grad_small, ce_got, parts = backward_all(
         att_got,
         ff_got,
         probs,
@@ -1669,6 +1631,16 @@
         grad_hidden,
         grad_embedding,
         normed_two,
+        turned(attention_weight),
+        turned(attention_moment),
+        feedforward_weight,
+        feedforward_moment,
+        att_rank,
+        ff_rank,
+        head_bias_weight,
+        head_bias_moment,
+        inner_bias_weight,
+        inner_bias_moment,
         bias_got,
         swapped(norm_weight),
         inputs,
@@ -1681,106 +1653,41 @@
         inverse_one,
         inverse_two,
     )
-    ce_total = ce_got[0, 0]
-    (
-        att_grad,
-        att_moment,
-        ff_grad,
-        ff_moment,
-        new_memory,
-        embedding_grad,
-        embedding_moment_next,
-        head_grad,
-        head_moment,
-        inner_grad,
-        inner_moment,
-        norm_grad,
-        norm_moment_next,
-        part,
-    ) = moments(
+    updated = update(
         turned(attention_weight),
         turned(attention_moment),
+        turned(attention_average),
         feedforward_weight,
         feedforward_moment,
+        feedforward_average,
         new_memory,
         grad_attention,
         grad_feedforward,
         grad_small,
+        parts,
         att_rank,
         ff_rank,
+        embedding_weight,
         embedding_moment,
+        embedding_average,
         head_bias_weight,
         head_bias_moment,
+        head_bias_average,
         inner_bias_weight,
         inner_bias_moment,
+        inner_bias_average,
+        swapped(norm_weight),
         swapped(norm_moment),
-    )
-    parts = exchange(part)
-    (
-        att_next,
-        att_average,
-        ff_next,
-        ff_average,
-        head_next,
-        head_average,
-        inner_next,
-        inner_average,
-        embedding_next,
-        embedding_average_next,
-        norm_next,
-        norm_average_next,
-    ) = new_weights(
-        turned(attention_weight),
-        att_grad,
-        att_moment,
-        turned(attention_average),
-        feedforward_weight,
-        ff_grad,
-        ff_moment,
-        feedforward_average,
-        head_bias_weight,
-        head_grad,
-        head_moment,
-        head_bias_average,
-        inner_bias_weight,
-        inner_grad,
-        inner_moment,
-        inner_bias_average,
-        embedding_weight,
-        embedding_grad,
-        embedding_moment_next,
-        embedding_average,
-        swapped(norm_weight),
-        norm_grad,
-        norm_moment_next,
         swapped(norm_average),
-        parts,
     )
     return (
-        ce_total,
+        ce_got[0, 0],
         valid_count,
-        new_memory,
-        turned(att_grad),
-        turned(att_next),
-        turned(att_moment),
-        turned(att_average),
-        ff_grad,
-        ff_next,
-        ff_moment,
-        ff_average,
-        embedding_next,
-        embedding_moment_next,
-        embedding_average_next,
-        head_next,
-        head_moment,
-        head_average,
-        inner_next,
-        inner_moment,
-        inner_average,
-        swapped(norm_grad),
-        swapped(norm_next),
-        swapped(norm_moment_next),
-        swapped(norm_average_next),
+        updated[8],
+        *[turned(value) for value in updated[0:4]],
+        *updated[4:8],
+        *updated[9:18],
+        *[swapped(value) for value in updated[18:22]],
     )
 
 

time: 211 us -> 199 us (0.943)
  Pallas kernels: 201 us -> 190 us
    pallas_call x3 -> x1, Pallas kernels: 28.6 us -> 14.5 us  [update(): pl.pallas_call(update_kernel, out_shape=[jax.ShapeDtypeStruct(s, F32) for...]
    pallas_call x1, Pallas kernels: 95.5 us -> 98.4 us  [backward_all(): pl.pallas_call(backward_step, out_shape=[jax.ShapeDtypeStruct(s, t) for s...]
where the time goes in v1:
time: 199 us; the launch traced here: 196 us
  Pallas kernels  190 us (95%)
  local copies, waits for them, and re-layouts  3.67 us (2%)
    pallas_call x1, Pallas kernels, backward_all(): pl.pallas_call(backward_step, out_shape=[jax.ShapeDtypeStruct(s, t) for s...  98.4 us
    pallas_call x1, Pallas kernels, forward_all(): pl.pallas_call(forward_step, out_shape=[jax.ShapeDtypeStruct(s, t) for _,...  76.7 us
    pallas_call x1, Pallas kernels, update(): pl.pallas_call(update_kernel, out_shape=[jax.ShapeDtypeStruct(s, F32) for...  14.5 us

profile of v1, /device:TPU:1, one launch (start us, length us, event | category | flops | bytes accessed | tf_op | source)
XLA Modules:
  0.0 195.5 jit_solution(7187457836269083877)
XLA Ops:
  0.7 0.7 convert_reduce_fusion
  1.4 0.6 reshape.52.att_rank_ref.refs_11_
  2.0 0.7 convert_element_type.12
  2.7 0.7 copy.66
  3.4 76.7 %forward_all.1 = (bf16[2,5,2,4,64,512]{5,4,3,2,1,0:T(8,128)(2,1)}, bf16[2,2,2,4,512,256]{5,4,3,2,1,0:T(8,128)(2,1)}, bf16[2,4,512,512]{3,2,1,0:T(8,128)(2,1)}, f...) custom-call(f32[2,5,64,512]{3,2,1,0:T(8,128)} %bitcast.17, ...), custom_call_target="tpu_custom_call" | custom-call | tf_op jit(solution)/shard_map/forward_all/pallas_call | solution.py:608
  80.0 1.2 slice.7
  81.2 98.4 %backward_all.1 = (bf16[2,5,64,512]{3,2,1,0:T(8,128)(2,1)}, bf16[2,2,512,256]{3,2,1,0:T(8,128)(2,1)}, bf16[4,2,64,512]{3,2,1,0:T(8,128)(2,1)}, f32[8,128]{1,0:T(8,128)}, f32[8,8,128]{2,1,0:T(8,128)}) custom-call(bf16[2,5,2,4,64,512]{5,4,3,2,1,0:T(8,128)(2,1)} %get-tuple-element.68.att_hbm, bf16[2,2,2,4,512,256]{5,4,3,2,1,0:T(8,128)(2,1)} %get-tuple-element.69.ff_hbm, ...), custom_call_target="tpu_custom_call" | custom-call | tf_op jit(solution)/shard_map/backward_all/pallas_call | solution.py:1367
  179.6 1.2 slice.6
  180.8 14.5 %update.1 = (f32[2,5,64,512]{3,2,1,0:T(8,128)}, f32[2,5,64,512]{3,2,1,0:T(8,128)}, f32[2,5,64,512]{3,2,1,0:T(8,128)}, f32[2,5,64,512]{3,2,1,0:T(8,128)}, f32[2,2...) custom-call(f32[2,5,64,512]{3,2,1,0:T(8,128)} %bitcast.19, ...), custom_call_target="tpu_custom_call" | custom-call | tf_op jit(solution)/shard_map/update/pallas_call | solution.py:1534

commit v2 on v1

--- a/solution.py
+++ b/solution.py
@@ -461,8 +461,10 @@
             slot = h % 2
             mine = lane_head == h % 4
             lanes = pl.ds(pl.multiple_of(group * 256, 256), 256)
-            query_u = jnp.where(mine, query_u_out[layer, :, lanes].astype(F32), 0.0).astype(BF16)
-            query_w = jnp.where(mine, query_w_out[layer, :, lanes].astype(F32), 0.0).astype(BF16)
+            query_u = query_u_out[layer, :, lanes].astype(F32) * SCALE
+            query_u = jnp.where(mine, query_u, 0.0).astype(BF16)
+            query_w = query_w_out[layer, :, lanes].astype(F32) * SCALE
+            query_w = jnp.where(mine, query_w, 0.0).astype(BF16)
             score_ref[...] = dot_nn(query_w, rel_ref[lanes, :])
 
             @pl.when(h >= 2)
@@ -475,10 +477,11 @@
             for b in range(0, OWN, ROWS):
                 rows = slice(b, b + ROWS)
                 moved = pltpu.roll(score_ref[rows, :], b, 1, stride=1, stride_axis=0)
-                score = (prob_ref[slot, rows, :] + moved) * SCALE
-                key_id = lax.broadcasted_iota(jnp.int32, (ROWS, KLEN), 1)
-                query_id = lax.broadcasted_iota(jnp.int32, (ROWS, KLEN), 0) + (offset + b + SEG)
-                score = jnp.where(key_id <= query_id, score, -1e30)
+                score = prob_ref[slot, rows, :] + moved
+                key_id = lax.broadcasted_iota(jnp.int32, (ROWS, SEG), 1)
+                query_id = lax.broadcasted_iota(jnp.int32, (ROWS, SEG), 0) + (offset + b)
+                near = jnp.where(key_id <= query_id, score[:, SEG:], -1e30)
+                score = jnp.concatenate([score[:, :SEG], near], axis=1)
                 expo = jnp.exp(score - jnp.max(score, axis=-1, keepdims=True))
                 prob = expo * (1.0 / jnp.sum(expo, axis=-1, keepdims=True))
                 prob_ref[slot, rows, :] = prob
@@ -1392,10 +1395,14 @@
         parts_ref,
         att_rank_ref,
         ff_rank_ref,
+        ce_ref,
+        count_ref,
         *rest,
-    ) = refs[:25]
+    ) = refs[:27]
     embedding, head, inner, norm = (rest[3 * i : 3 * i + 3] for i in range(4))
-    outs = refs[25:47]
+    outs = refs[27:51]
+    outs[22][...] = ce_ref[0:1, 0:1]
+    outs[23][...] = count_ref[0:1, 0:1]
     att_outs, ff_outs, new_memory_out = outs[0:4], outs[4:8], outs[8]
     embedding_outs, head_outs, inner_outs, norm_outs = (
         outs[9:12],
@@ -1403,8 +1410,8 @@
         outs[15:18],
         outs[18:22],
     )
-    att, ff = refs[47:51], refs[51:55]
-    att_rank, ff_rank, memory_ref, load_sem, store_sem, memory_sem = refs[55:]
+    att, ff = refs[51:55], refs[55:59]
+    att_rank, ff_rank, memory_ref, load_sem, store_sem, memory_sem = refs[59:]
     loads, stores = [], []
     for l in range(2):
         for k, (sources, targets) in enumerate(
@@ -1530,14 +1537,14 @@
 def update(*operands):
     att, ff = (2, 5, HD, D), (2, 2, D, 256)
     shapes = [att] * 4 + [ff] * 4
-    rest = [(VOCAB, D)] * 3 + [(2, 2, HD)] * 3 + [(2, 256)] * 3 + [(5, 2, D)] * 4
+    rest = [(VOCAB, D)] * 3 + [(2, 2, HD)] * 3 + [(2, 256)] * 3 + [(5, 2, D)] * 4 + [(1, 1)] * 2
     return pl.pallas_call(
         update_kernel,
         out_shape=[jax.ShapeDtypeStruct(s, F32) for s in shapes]
         + [jax.ShapeDtypeStruct((2, 4, SEG, D), BF16)]
         + [jax.ShapeDtypeStruct(s, F32) for s in rest],
-        in_specs=[ANY_SPEC] * 7 + [VMEM_SPEC] * 18,
-        out_specs=[ANY_SPEC] * 9 + [VMEM_SPEC] * 13,
+        in_specs=[ANY_SPEC] * 7 + [VMEM_SPEC] * 20,
+        out_specs=[ANY_SPEC] * 9 + [VMEM_SPEC] * 15,
         scratch_shapes=[pltpu.VMEM(att, F32)] * 4
         + [pltpu.VMEM(ff, F32)] * 4
         + [
@@ -1621,7 +1628,6 @@
         swapped(norm_weight),
         table,
     )
-    valid_count = count_got[0, 0]
     grad_attention, grad_feedforward, grad_small, ce_got, parts = backward_all(
         att_got,
         ff_got,
@@ -1667,6 +1673,8 @@
         parts,
         att_rank,
         ff_rank,
+        ce_got,
+        count_got,
         embedding_weight,
         embedding_moment,
         embedding_average,
@@ -1681,8 +1689,8 @@
         swapped(norm_average),
     )
     return (
-        ce_got[0, 0],
-        valid_count,
+        updated[22].reshape(()),
+        updated[23].reshape(()),
         updated[8],
         *[turned(value) for value in updated[0:4]],
         *updated[4:8],

time: 199 us -> 197 us (0.990)
  local copies, waits for them, and re-layouts: 3.67 us -> 1.29 us
    slice x2 -> x0, local copies, waits for them, and re-layouts: 2.38 us -> none  [the longest x1 1.19 us: body(): ce_got[0, 0]]
where the time goes in v2:
time: 197 us; the launch traced here: 193 us
  Pallas kernels  190 us (96%)
    pallas_call x1, Pallas kernels, backward_all(): pl.pallas_call(backward_step, out_shape=[jax.ShapeDtypeStruct(s, t) for s...  98.6 us
    pallas_call x1, Pallas kernels, forward_all(): pl.pallas_call(forward_step, out_shape=[jax.ShapeDtypeStruct(s, t) for _,...  76.5 us
    pallas_call x1, Pallas kernels, update(): pl.pallas_call(update_kernel, out_shape=[jax.ShapeDtypeStruct(s, F32) for...  14.6 us

profile of v2, /device:TPU:1, one launch (start us, length us, event | category | flops | bytes accessed | tf_op | source)
XLA Modules:
  0.0 193.3 jit_solution(18168025050348477806)
XLA Ops:
  0.7 0.7 convert_reduce_fusion
  1.4 0.6 reshape.60.att_rank_ref.refs_11_
  2.0 0.7 convert_element_type.12
  2.7 0.7 copy.66
  3.4 76.5 %forward_all.1 = (bf16[2,5,2,4,64,512]{5,4,3,2,1,0:T(8,128)(2,1)}, bf16[2,2,2,4,512,256]{5,4,3,2,1,0:T(8,128)(2,1)}, bf16[2,4,512,512]{3,2,1,0:T(8,128)(2,1)}, f...) custom-call(f32[2,5,64,512]{3,2,1,0:T(8,128)} %bitcast.17, ...), custom_call_target="tpu_custom_call" | custom-call | tf_op jit(solution)/shard_map/forward_all/pallas_call | solution.py:611
  79.9 98.6 %backward_all.1 = (bf16[2,5,64,512]{3,2,1,0:T(8,128)(2,1)}, bf16[2,2,512,256]{3,2,1,0:T(8,128)(2,1)}, bf16[4,2,64,512]{3,2,1,0:T(8,128)(2,1)}, f32[8,128]{1,0:T(8,128)}, f32[8,8,128]{2,1,0:T(8,128)}) custom-call(bf16[2,5,2,4,64,512]{5,4,3,2,1,0:T(8,128)(2,1)} %get-tuple-element.71.att_hbm, bf16[2,2,2,4,512,256]{5,4,3,2,1,0:T(8,128)(2,1)} %get-tuple-element.72.ff_hbm, ...), custom_call_target="tpu_custom_call" | custom-call | tf_op jit(solution)/shard_map/backward_all/pallas_call | solution.py:1370
  178.5 14.6 %update.1 = (f32[2,5,64,512]{3,2,1,0:T(8,128)}, f32[2,5,64,512]{3,2,1,0:T(8,128)}, f32[2,5,64,512]{3,2,1,0:T(8,128)}, f32[2,5,64,512]{3,2,1,0:T(8,128)}, f32[2,2...) custom-call(f32[2,5,64,512]{3,2,1,0:T(8,128)} %bitcast.19, ...), custom_call_target="tpu_custom_call" | custom-call | tf_op jit(solution)/shard_map/update/pallas_call | solution.py:1541
